TPU v7x, 32 devices: a whole 2x2x4 slice. The times are simulated.
32 devices in a mesh: depth: 4 (over z), row: 8 (over y, x, core).
Axes of the slice: x: 2, y: 2, z: 4, core: 2. Of those that a mesh axis runs over, the one named last changes fastest.
Arguments:
- volume: float32 [192, 512, 2048], P('depth', 'row'), may hold values from -6 to 6
- transfer: float32 [8], replicated, may hold values from 0.3 to 1.2
Outputs:
- image: float32 [4, 512, 2048], P(None, 'row', 'depth')
All inputs are finite; a program needn't handle non-finite values.
Results may differ from a plain program's by a relative error of at most 0.0003.
Values sent between devices are 32-bit elements; how exact they have to be, the bound alone decides.
No kernel may reach another device: no remote copies, remote signals or barrier semaphores. Data moves between devices by JAX's collectives and lax.ppermute only.
A program may use at most 192 MiB of HBM per device.

v0:
```python
import jax
import jax.numpy as jnp
from jax import lax
from jax.sharding import PartitionSpec as P


def with_halo(cells, sides, width):
    for axis, dim in sides:
        count = lax.axis_size(axis)
        ends = count - 1
        head = lax.slice_in_dim(cells, 0, width, axis=dim)
        tail = lax.slice_in_dim(cells, cells.shape[dim] - width, cells.shape[dim], axis=dim)
        cells = jnp.concatenate(
            [
                lax.ppermute(tail, axis, [(i, (i + 1) % count) for i in range(ends)]),
                cells,
                lax.ppermute(head, axis, [((i + 1) % count, i) for i in range(ends)]),
            ],
            axis=dim,
        )
    return cells


def partner(value, axis, distance):
    mask = 2**distance
    pairs = [(source, source ^ mask) for source in range(lax.axis_size(axis))]
    return lax.ppermute(value, axis, pairs)


def slope_cols(center):
    zero_col = jnp.zeros_like(center[..., :1])
    right = jnp.concatenate([center[..., 1:], zero_col], -1)
    left = jnp.concatenate([zero_col, center[..., :-1]], -1)
    return 0.5 * (right - left)


def emit(framed, transfer, slices):
    center = framed[1:-1, 1:-1, :]
    slope_depth = 0.5 * (framed[2:, 1:-1, :] - framed[:-2, 1:-1, :])
    slope_row = 0.5 * (framed[1:-1, 2:, :] - framed[1:-1, :-2, :])
    slope_col = slope_cols(center)
    inverse = lax.rsqrt(
        slope_depth * slope_depth + slope_row * slope_row + slope_col * slope_col + 1.0
    )
    lambert = jnp.abs((slope_depth + 2.0 * slope_row + 2.0 * slope_col) * inverse) / 3.0
    ambient = 0.5 * transfer[7]
    shading = ambient + (1.0 - ambient) * lambert
    depth_term = 2.0 * transfer[6] / slices * jax.nn.softplus(center)
    opacity = -jnp.expm1(-depth_term)
    tinting = jax.nn.sigmoid(2.0 * center)
    weight = shading * opacity
    emitted = jnp.stack(
        [(transfer[channel] + transfer[3 + channel] * tinting) * weight for channel in range(3)]
    )
    return (emitted, depth_term)


def on_device(volume, transfer):
    local_slices, local_rows, columns = volume.shape
    groups = lax.axis_size("depth")
    slices = local_slices * groups
    padded = with_halo(volume, (("depth", 0), ("row", 1)), 1)
    steps = local_slices // 8

    def march(carry, index):
        color, depth_acc = carry
        slab = lax.dynamic_slice_in_dim(padded, index * 8, 10, 0)
        emitted, depth_term = emit(slab, transfer, slices)
        before = jnp.cumsum(depth_term, 0) - depth_term
        passing = jnp.exp(-(depth_acc[None] + before))
        color = color + jnp.sum(passing[None] * emitted, 1)
        depth_acc = depth_acc + jnp.sum(depth_term, 0)
        return ((color, depth_acc), None)

    start_color = jnp.zeros((3, local_rows, columns), jnp.float32)
    start_depth = jnp.zeros((local_rows, columns), jnp.float32)
    (color, depth_acc), unused = lax.scan(
        march, (start_color, start_depth), jnp.arange(steps, dtype=jnp.int32)
    )
    partial_image = jnp.concatenate([color, depth_acc[None]], 0)
    held = partial_image
    block_width = columns // groups
    levels = groups.bit_length() - 1
    for level in range(levels):
        count = held.shape[2] // block_width
        shaped = held.reshape(4, local_rows, count // 2, 2, block_width)
        my_bit = lax.axis_index("depth") >> level & 1
        is_front = my_bit == 0
        keep = jnp.where(is_front, shaped[:, :, :, 0, :], shaped[:, :, :, 1, :])
        sending = jnp.where(is_front, shaped[:, :, :, 1, :], shaped[:, :, :, 0, :])
        received = partner(sending, "depth", level)
        front = jnp.where(is_front, keep, received)
        back = jnp.where(is_front, received, keep)
        merged_color = front[:3] + jnp.exp(-front[3])[None] * back[:3]
        merged_depth = front[3] + back[3]
        held = jnp.concatenate([merged_color, merged_depth[None]], 0).reshape(
            4, local_rows, count // 2 * block_width
        )
    return jnp.concatenate([held[:3], -jnp.expm1(-held[3:4])], 0)


def solution(mesh):
    in_specs = (P("depth", "row", None), P())
    out_specs = P(None, "row", "depth")
    return jax.shard_map(
        on_device, mesh=mesh, in_specs=in_specs, out_specs=out_specs, check_vma=False
    )
```

profile of v0, /device:TPU:4, one launch (start us, length us, event | category | flops | bytes accessed | tf_op | source)
XLA Modules:
  0.0 476.1 jit_solution(11783326489887922762)
XLA Ops:
  0.0 1.3 fusion.15
  1.3 3.5 collective-permute-start
  4.8 1.3 collective-permute-start.1
  6.1 9.8 %collective-permute-done = f32[1,64,2048]{2,1,0:T(8,128)S(1)} collective-permute-done((f32[1,64,2048]{2,1,0:T(8,128)S(1)}, f32[1,64,2048]{2,1,0:T(8,128)S(1)}, u32[]{:S(2)}, u32[]{:S(2)}) %collective-permute-start) | collective-permute-done | bytes 524320 | tf_op jit(solution)/shard_map/ppermute | solution.py:15
  16.0 10.6 %constant_dynamic-update-slice_fusion.1 = f32[50,64,2048]{2,1,0:T(8,128)S(1)} fusion(f32[50,64,2048]{2,1,0:T(8,128)S(1)} %constant_dynamic-update-slice_fusion.2, f32[48,64,2048]{2,1,0:T(8,128)} %param.4), kind=kLoop, calls=%fused_computation.45 | loop fusion | bytes 50331648
  26.7 0.8 fusion.14
  27.5 1.9 collective-permute-start.2
  29.4 5.9 %copy-done.2 = f32[50,64,2048]{2,1,0:T(8,128)} copy-done((f32[50,64,2048]{2,1,0:T(8,128)}, f32[50,64,2048]{2,1,0:T(8,128)S(1)}, u32[]{:S(2)}) %copy-start.2) | copy-done | bytes 26214424
  35.3 1.9 collective-permute-start.3
  37.3 0.6 fusion.17
  39.2 3.5 collective-permute-done.3
  42.7 20.7 %pad_maximum_fusion = f32[50,66,2048]{2,1,0:T(8,128)} fusion(f32[50,1,2048]{2,1,0:T(1,128)} %collective-permute-done.3, f32[50,64,2048]{2,1,0:T(8,128)} %copy-done.2, f32[50,1,2048]{2,1,0:T(1,128)S(1)} %collective-permute-done.2), kind=kLoop, calls=%fused_computation.17 | loop fusion | flops 13516800 | bytes 54067200 | tf_op jit(solution)/shard_map/concatenate | solution.py:13
  63.4 344.8 %while.16 = (s32[]{:T(128)}, f32[3,64,2048]{2,1,0:T(8,128)S(1)}, f32[64,2048]{1,0:T(8,128)S(1)}, f32[]{:T(128)}, s32[6]{0:T(128)S(1)}, /*index=5*/f32[50,66,2048...) while((s32[]{:T(128)}, f32[3,64,2048]{2,1,0:T(8,128)S(1)}, ...), condition=%wide.region_4.5_spmd.clone, body=%wide.region_0.4_spmd.clone.sunk | while | flops 86507528 | bytes 139449296 | solution.py:77
  64.6 8.3 %fusion.25 = (f32[8,64,2047]{2,1,0:T(8,128)}, f32[8,64,2047]{2,1,0:T(8,128)}) fusion(f32[50,66,2048]{2,1,0:T(8,128)} %get-tuple-element.331, s32[]{:T(128)S(6)} %add.284, s32[]{:T(128)S(6)} %add.285), kind=kLoop, calls=%fused_computation.50.clone.1 | loop fusion | bytes 16769032 | tf_op jit(solution)/shard_map/while/body/eval_jaxpr/slice | solution.py:32
  72.9 0.7 fusion.24
  73.6 18.1 %multiply_bitcast_fusion.5 = (f32[1,8,64,2048]{3,2,1,0:T(8,128)}, f32[8,64,2048]{2,1,0:T(8,128)S(1)}) fusion(f32[]{:T(128)} %bitcast.73, f32[]{:T(128)} %bitcast.74, f32[50,66,2048]{2,1,0:T(8,128)} %get-tuple-element.331, s32[]{:T(128)S(6)} %add.284, s32[]{:T(128)S(6)} %add.285, f32[]{:T(128)} %get-tuple-element.329, f32[]{:T(128)} %get-tuple-element.334, ...), kind=kLoop, calls=%fused_computation.9.clone.1 | loop fusion | flops 36700160 | bytes 37744680 | tf_op jit(solution)/shard_map/while/body/eval_jaxpr/stack | solution.py:52
  91.7 10.4 %multiply_bitcast_fusion.6 = (f32[1,8,64,2048]{3,2,1,0:T(8,128)}, f32[1,8,64,2048]{3,2,1,0:T(8,128)}, f32[64,2048]{1,0:T(8,128)S(1)}) fusion(f32[8,64,2048]{2,1,0:T(8,128)S(1)} %get-tuple-element.285, f32[]{:T(128)} %bitcast.76, f32[]{:T(128)} %bitcast.77, f32[50,66,2048]{2,1,0:T(8,128)} %get-tuple-element.331, s32[]{:T(128)S(6)} %add.284, ...), kind=kLoop, calls=%fused_computation.8.clone.1 | loop fusion | flops 18743296 | bytes 17301532 | tf_op jit(solution)/shard_map/while/body/eval_jaxpr/stack | solution.py:52
  102.3 13.1 %negate_exponential_fusion.3 = f32[8,64,2048]{2,1,0:T(8,128)S(1)} fusion(f32[64,2048]{1,0:T(8,128)S(1)} %get-tuple-element.294, f32[50,66,2048]{2,1,0:T(8,128)} %get-tuple-element.331, s32[]{:T(128)S(6)} %add.284, s32[]{:T(128)S(6)} %add.285, f32[]{:T(128)} %get-tuple-element.329), kind=kOutput, calls=%fused_computation.12.clone.1 | output fusion | flops 17825792 | bytes 8913416 | tf_op jit(solution)/shard_map/while/body/eval_jaxpr/jit(cumsum)/reduce_window_sum | solution.py:69
  115.4 4.0 fusion.27
  120.0 0.6 dynamic_slice.18
  121.2 8.3 %fusion.25 = (f32[8,64,2047]{2,1,0:T(8,128)}, f32[8,64,2047]{2,1,0:T(8,128)}) fusion(f32[50,66,2048]{2,1,0:T(8,128)} %get-tuple-element.331, s32[]{:T(128)S(6)} %add.284, s32[]{:T(128)S(6)} %add.285), kind=kLoop, calls=%fused_computation.50.clone.1 | loop fusion | bytes 16769032 | tf_op jit(solution)/shard_map/while/body/eval_jaxpr/slice | solution.py:32
  129.5 0.7 fusion.24
  130.2 18.1 %multiply_bitcast_fusion.5 = (f32[1,8,64,2048]{3,2,1,0:T(8,128)}, f32[8,64,2048]{2,1,0:T(8,128)S(1)}) fusion(f32[]{:T(128)} %bitcast.73, f32[]{:T(128)} %bitcast.74, f32[50,66,2048]{2,1,0:T(8,128)} %get-tuple-element.331, s32[]{:T(128)S(6)} %add.284, s32[]{:T(128)S(6)} %add.285, f32[]{:T(128)} %get-tuple-element.329, f32[]{:T(128)} %get-tuple-element.334, ...), kind=kLoop, calls=%fused_computation.9.clone.1 | loop fusion | flops 36700160 | bytes 37744680 | tf_op jit(solution)/shard_map/while/body/eval_jaxpr/stack | solution.py:52
  148.3 10.4 %multiply_bitcast_fusion.6 = (f32[1,8,64,2048]{3,2,1,0:T(8,128)}, f32[1,8,64,2048]{3,2,1,0:T(8,128)}, f32[64,2048]{1,0:T(8,128)S(1)}) fusion(f32[8,64,2048]{2,1,0:T(8,128)S(1)} %get-tuple-element.285, f32[]{:T(128)} %bitcast.76, f32[]{:T(128)} %bitcast.77, f32[50,66,2048]{2,1,0:T(8,128)} %get-tuple-element.331, s32[]{:T(128)S(6)} %add.284, ...), kind=kLoop, calls=%fused_computation.8.clone.1 | loop fusion | flops 18743296 | bytes 17301532 | tf_op jit(solution)/shard_map/while/body/eval_jaxpr/stack | solution.py:52
  158.9 14.0 %negate_exponential_fusion.3 = f32[8,64,2048]{2,1,0:T(8,128)S(1)} fusion(f32[64,2048]{1,0:T(8,128)S(1)} %get-tuple-element.294, f32[50,66,2048]{2,1,0:T(8,128)} %get-tuple-element.331, s32[]{:T(128)S(6)} %add.284, s32[]{:T(128)S(6)} %add.285, f32[]{:T(128)} %get-tuple-element.329), kind=kOutput, calls=%fused_computation.12.clone.1 | output fusion | flops 17825792 | bytes 8913416 | tf_op jit(solution)/shard_map/while/body/eval_jaxpr/jit(cumsum)/reduce_window_sum | solution.py:69
  172.9 4.0 fusion.27
  177.5 0.6 dynamic_slice.18
  178.7 8.4 %fusion.25 = (f32[8,64,2047]{2,1,0:T(8,128)}, f32[8,64,2047]{2,1,0:T(8,128)}) fusion(f32[50,66,2048]{2,1,0:T(8,128)} %get-tuple-element.331, s32[]{:T(128)S(6)} %add.284, s32[]{:T(128)S(6)} %add.285), kind=kLoop, calls=%fused_computation.50.clone.1 | loop fusion | bytes 16769032 | tf_op jit(solution)/shard_map/while/body/eval_jaxpr/slice | solution.py:32
  187.1 0.7 fusion.24
  187.8 18.0 %multiply_bitcast_fusion.5 = (f32[1,8,64,2048]{3,2,1,0:T(8,128)}, f32[8,64,2048]{2,1,0:T(8,128)S(1)}) fusion(f32[]{:T(128)} %bitcast.73, f32[]{:T(128)} %bitcast.74, f32[50,66,2048]{2,1,0:T(8,128)} %get-tuple-element.331, s32[]{:T(128)S(6)} %add.284, s32[]{:T(128)S(6)} %add.285, f32[]{:T(128)} %get-tuple-element.329, f32[]{:T(128)} %get-tuple-element.334, ...), kind=kLoop, calls=%fused_computation.9.clone.1 | loop fusion | flops 36700160 | bytes 37744680 | tf_op jit(solution)/shard_map/while/body/eval_jaxpr/stack | solution.py:52
  205.8 10.4 %multiply_bitcast_fusion.6 = (f32[1,8,64,2048]{3,2,1,0:T(8,128)}, f32[1,8,64,2048]{3,2,1,0:T(8,128)}, f32[64,2048]{1,0:T(8,128)S(1)}) fusion(f32[8,64,2048]{2,1,0:T(8,128)S(1)} %get-tuple-element.285, f32[]{:T(128)} %bitcast.76, f32[]{:T(128)} %bitcast.77, f32[50,66,2048]{2,1,0:T(8,128)} %get-tuple-element.331, s32[]{:T(128)S(6)} %add.284, ...), kind=kLoop, calls=%fused_computation.8.clone.1 | loop fusion | flops 18743296 | bytes 17301532 | tf_op jit(solution)/shard_map/while/body/eval_jaxpr/stack | solution.py:52
  216.4 14.5 %negate_exponential_fusion.3 = f32[8,64,2048]{2,1,0:T(8,128)S(1)} fusion(f32[64,2048]{1,0:T(8,128)S(1)} %get-tuple-element.294, f32[50,66,2048]{2,1,0:T(8,128)} %get-tuple-element.331, s32[]{:T(128)S(6)} %add.284, s32[]{:T(128)S(6)} %add.285, f32[]{:T(128)} %get-tuple-element.329), kind=kOutput, calls=%fused_computation.12.clone.1 | output fusion | flops 17825792 | bytes 8913416 | tf_op jit(solution)/shard_map/while/body/eval_jaxpr/jit(cumsum)/reduce_window_sum | solution.py:69
  230.9 4.0 fusion.27
  235.4 0.6 dynamic_slice.18
  236.6 8.3 %fusion.25 = (f32[8,64,2047]{2,1,0:T(8,128)}, f32[8,64,2047]{2,1,0:T(8,128)}) fusion(f32[50,66,2048]{2,1,0:T(8,128)} %get-tuple-element.331, s32[]{:T(128)S(6)} %add.284, s32[]{:T(128)S(6)} %add.285), kind=kLoop, calls=%fused_computation.50.clone.1 | loop fusion | bytes 16769032 | tf_op jit(solution)/shard_map/while/body/eval_jaxpr/slice | solution.py:32
  245.0 0.7 fusion.24
  245.6 17.9 %multiply_bitcast_fusion.5 = (f32[1,8,64,2048]{3,2,1,0:T(8,128)}, f32[8,64,2048]{2,1,0:T(8,128)S(1)}) fusion(f32[]{:T(128)} %bitcast.73, f32[]{:T(128)} %bitcast.74, f32[50,66,2048]{2,1,0:T(8,128)} %get-tuple-element.331, s32[]{:T(128)S(6)} %add.284, s32[]{:T(128)S(6)} %add.285, f32[]{:T(128)} %get-tuple-element.329, f32[]{:T(128)} %get-tuple-element.334, ...), kind=kLoop, calls=%fused_computation.9.clone.1 | loop fusion | flops 36700160 | bytes 37744680 | tf_op jit(solution)/shard_map/while/body/eval_jaxpr/stack | solution.py:52
  263.6 10.4 %multiply_bitcast_fusion.6 = (f32[1,8,64,2048]{3,2,1,0:T(8,128)}, f32[1,8,64,2048]{3,2,1,0:T(8,128)}, f32[64,2048]{1,0:T(8,128)S(1)}) fusion(f32[8,64,2048]{2,1,0:T(8,128)S(1)} %get-tuple-element.285, f32[]{:T(128)} %bitcast.76, f32[]{:T(128)} %bitcast.77, f32[50,66,2048]{2,1,0:T(8,128)} %get-tuple-element.331, s32[]{:T(128)S(6)} %add.284, ...), kind=kLoop, calls=%fused_computation.8.clone.1 | loop fusion | flops 18743296 | bytes 17301532 | tf_op jit(solution)/shard_map/while/body/eval_jaxpr/stack | solution.py:52
  274.1 13.7 %negate_exponential_fusion.3 = f32[8,64,2048]{2,1,0:T(8,128)S(1)} fusion(f32[64,2048]{1,0:T(8,128)S(1)} %get-tuple-element.294, f32[50,66,2048]{2,1,0:T(8,128)} %get-tuple-element.331, s32[]{:T(128)S(6)} %add.284, s32[]{:T(128)S(6)} %add.285, f32[]{:T(128)} %get-tuple-element.329), kind=kOutput, calls=%fused_computation.12.clone.1 | output fusion | flops 17825792 | bytes 8913416 | tf_op jit(solution)/shard_map/while/body/eval_jaxpr/jit(cumsum)/reduce_window_sum | solution.py:69
  287.9 4.0 fusion.27
  292.4 0.6 dynamic_slice.18
  293.7 8.4 %fusion.25 = (f32[8,64,2047]{2,1,0:T(8,128)}, f32[8,64,2047]{2,1,0:T(8,128)}) fusion(f32[50,66,2048]{2,1,0:T(8,128)} %get-tuple-element.331, s32[]{:T(128)S(6)} %add.284, s32[]{:T(128)S(6)} %add.285), kind=kLoop, calls=%fused_computation.50.clone.1 | loop fusion | bytes 16769032 | tf_op jit(solution)/shard_map/while/body/eval_jaxpr/slice | solution.py:32
  302.0 0.7 fusion.24
  302.7 18.4 %multiply_bitcast_fusion.5 = (f32[1,8,64,2048]{3,2,1,0:T(8,128)}, f32[8,64,2048]{2,1,0:T(8,128)S(1)}) fusion(f32[]{:T(128)} %bitcast.73, f32[]{:T(128)} %bitcast.74, f32[50,66,2048]{2,1,0:T(8,128)} %get-tuple-element.331, s32[]{:T(128)S(6)} %add.284, s32[]{:T(128)S(6)} %add.285, f32[]{:T(128)} %get-tuple-element.329, f32[]{:T(128)} %get-tuple-element.334, ...), kind=kLoop, calls=%fused_computation.9.clone.1 | loop fusion | flops 36700160 | bytes 37744680 | tf_op jit(solution)/shard_map/while/body/eval_jaxpr/stack | solution.py:52
  321.0 10.4 %multiply_bitcast_fusion.6 = (f32[1,8,64,2048]{3,2,1,0:T(8,128)}, f32[1,8,64,2048]{3,2,1,0:T(8,128)}, f32[64,2048]{1,0:T(8,128)S(1)}) fusion(f32[8,64,2048]{2,1,0:T(8,128)S(1)} %get-tuple-element.285, f32[]{:T(128)} %bitcast.76, f32[]{:T(128)} %bitcast.77, f32[50,66,2048]{2,1,0:T(8,128)} %get-tuple-element.331, s32[]{:T(128)S(6)} %add.284, ...), kind=kLoop, calls=%fused_computation.8.clone.1 | loop fusion | flops 18743296 | bytes 17301532 | tf_op jit(solution)/shard_map/while/body/eval_jaxpr/stack | solution.py:52
  331.6 14.3 %negate_exponential_fusion.3 = f32[8,64,2048]{2,1,0:T(8,128)S(1)} fusion(f32[64,2048]{1,0:T(8,128)S(1)} %get-tuple-element.294, f32[50,66,2048]{2,1,0:T(8,128)} %get-tuple-element.331, s32[]{:T(128)S(6)} %add.284, s32[]{:T(128)S(6)} %add.285, f32[]{:T(128)} %get-tuple-element.329), kind=kOutput, calls=%fused_computation.12.clone.1 | output fusion | flops 17825792 | bytes 8913416 | tf_op jit(solution)/shard_map/while/body/eval_jaxpr/jit(cumsum)/reduce_window_sum | solution.py:69
  345.9 4.0 fusion.27
  350.5 0.6 dynamic_slice.18
  351.7 8.3 %fusion.25 = (f32[8,64,2047]{2,1,0:T(8,128)}, f32[8,64,2047]{2,1,0:T(8,128)}) fusion(f32[50,66,2048]{2,1,0:T(8,128)} %get-tuple-element.331, s32[]{:T(128)S(6)} %add.284, s32[]{:T(128)S(6)} %add.285), kind=kLoop, calls=%fused_computation.50.clone.1 | loop fusion | bytes 16769032 | tf_op jit(solution)/shard_map/while/body/eval_jaxpr/slice | solution.py:32
  360.0 0.7 fusion.24
  360.7 18.1 %multiply_bitcast_fusion.5 = (f32[1,8,64,2048]{3,2,1,0:T(8,128)}, f32[8,64,2048]{2,1,0:T(8,128)S(1)}) fusion(f32[]{:T(128)} %bitcast.73, f32[]{:T(128)} %bitcast.74, f32[50,66,2048]{2,1,0:T(8,128)} %get-tuple-element.331, s32[]{:T(128)S(6)} %add.284, s32[]{:T(128)S(6)} %add.285, f32[]{:T(128)} %get-tuple-element.329, f32[]{:T(128)} %get-tuple-element.334, ...), kind=kLoop, calls=%fused_computation.9.clone.1 | loop fusion | flops 36700160 | bytes 37744680 | tf_op jit(solution)/shard_map/while/body/eval_jaxpr/stack | solution.py:52
  378.8 10.4 %multiply_bitcast_fusion.6 = (f32[1,8,64,2048]{3,2,1,0:T(8,128)}, f32[1,8,64,2048]{3,2,1,0:T(8,128)}, f32[64,2048]{1,0:T(8,128)S(1)}) fusion(f32[8,64,2048]{2,1,0:T(8,128)S(1)} %get-tuple-element.285, f32[]{:T(128)} %bitcast.76, f32[]{:T(128)} %bitcast.77, f32[50,66,2048]{2,1,0:T(8,128)} %get-tuple-element.331, s32[]{:T(128)S(6)} %add.284, ...), kind=kLoop, calls=%fused_computation.8.clone.1 | loop fusion | flops 18743296 | bytes 17301532 | tf_op jit(solution)/shard_map/while/body/eval_jaxpr/stack | solution.py:52
  389.4 14.0 %negate_exponential_fusion.3 = f32[8,64,2048]{2,1,0:T(8,128)S(1)} fusion(f32[64,2048]{1,0:T(8,128)S(1)} %get-tuple-element.294, f32[50,66,2048]{2,1,0:T(8,128)} %get-tuple-element.331, s32[]{:T(128)S(6)} %add.284, s32[]{:T(128)S(6)} %add.285, f32[]{:T(128)} %get-tuple-element.329), kind=kOutput, calls=%fused_computation.12.clone.1 | output fusion | flops 17825792 | bytes 8913416 | tf_op jit(solution)/shard_map/while/body/eval_jaxpr/jit(cumsum)/reduce_window_sum | solution.py:69
  403.4 4.0 fusion.27
  408.1 2.5 concatenate.29
  410.6 2.0 constant_dynamic-update-slice_fusion.4
  413.2 2.7 fusion.16
  416.5 2.5 collective-permute-start.4
  419.0 22.8 %collective-permute-done.4 = f32[4,64,2,512]{3,2,1,0:T(2,128)S(1)} collective-permute-done((f32[4,64,2,512]{3,2,1,0:T(2,128)S(1)}, f32[4,64,2,512]{3,2,1,0:T(2,128)S(1)}, u32[]{:S(2)}, u32[]{:S(2)}) %collective-permute-start.4) | collective-permute-done | bytes 1048608 | tf_op jit(solution)/shard_map/ppermute | solution.py:27
  441.8 2.4 broadcast_select_fusion.3
  446.0 3.4 collective-permute-start.5
  449.4 24.0 %collective-permute-done.5 = f32[4,64,1,512]{3,2,1,0:T(1,128)S(1)} collective-permute-done((f32[4,64,1,512]{3,2,1,0:T(1,128)S(1)}, f32[4,64,1,512]{3,2,1,0:T(1,128)S(1)}, u32[]{:S(2)}, u32[]{:S(2)}) %collective-permute-start.5) | collective-permute-done | bytes 524320 | tf_op jit(solution)/shard_map/ppermute | solution.py:27
  473.4 0.9 broadcast_select_fusion.6
  475.3 0.8 pad_maximum_fusion.1
  (59 shorter events, 8.7 us)
Async XLA Ops:
  1.3 14.7 %collective-permute-start = (f32[1,64,2048]{2,1,0:T(8,128)S(1)}, f32[1,64,2048]{2,1,0:T(8,128)S(1)}, u32[]{:S(2)}, u32[]{:S(2)}) collective-permute-start(f32[1,64,2048]{2,1,0:T(8,128)S(1)} %get-tuple-element.197), channel_id=1, source_target_pairs={{0,8},{8,16},{16,24},{1,9},{9,17},{17,25},{2,10},{10,18},{18,26},{... | collective-permute-start | bytes 1572872 | tf_op jit(solution)/shard_map/ppermute | solution.py:15
  4.8 21.8 %collective-permute-start.1 = (f32[1,64,2048]{2,1,0:T(8,128)S(1)}, f32[1,64,2048]{2,1,0:T(8,128)S(1)}, u32[]{:S(2)}, u32[]{:S(2)}) collective-permute-start(f32[1,64,2048]{2,1,0:T(8,128)S(1)} %get-tuple-element.196), channel_id=1, source_target_pairs={{8,0},{16,8},{24,16},{9,1},{17,9},{25,17},{10,2},{18,10},{26,18},{... | collective-permute-start | bytes 1572872 | tf_op jit(solution)/shard_map/ppermute | solution.py:17
  16.0 21.3 %copy-start.3 = (f32[8]{0:T(128)S(1)}, f32[8]{0:T(128)}, u32[]{:S(2)}) copy-start(f32[8]{0:T(128)} %param.5) | copy-start | bytes 100
  26.7 8.6 %copy-start.2 = (f32[50,64,2048]{2,1,0:T(8,128)}, f32[50,64,2048]{2,1,0:T(8,128)S(1)}, u32[]{:S(2)}) copy-start(f32[50,64,2048]{2,1,0:T(8,128)S(1)} %constant_dynamic-update-slice_fusion) | copy-start | bytes 78643200
  27.5 11.7 %collective-permute-start.2 = (f32[50,1,2048]{2,1,0:T(1,128)S(1)}, f32[50,1,2048]{2,1,0:T(1,128)S(1)}, u32[]{:S(2)}, u32[]{:S(2)}) collective-permute-start(f32[50,1,2048]{2,1,0:T(1,128)S(1)} %get-tuple-element.194), channel_id=1, source_target_pairs={{0,1},{1,2},{2,3},{3,4},{4,5},{5,6},{6,7},{8,9},{9,10},{10,11},{11... | collective-permute-start | bytes 1228808 | tf_op jit(solution)/shard_map/ppermute | solution.py:15
  35.3 7.4 %collective-permute-start.3 = (f32[50,1,2048]{2,1,0:T(1,128)S(1)}, f32[50,1,2048]{2,1,0:T(1,128)}, u32[]{:S(2)}, u32[]{:S(2)}) collective-permute-start(f32[50,1,2048]{2,1,0:T(1,128)S(1)} %get-tuple-element.195), channel_id=1, source_target_pairs={{1,0},{2,1},{3,2},{4,3},{5,4},{6,5},{7,6},{9,8},{10,9},{11,10},{12... | collective-permute-start | bytes 1228808 | tf_op jit(solution)/shard_map/ppermute | solution.py:17
  102.3 13.2 %copy-start = (f32[1,8,64,2048]{3,2,1,0:T(8,128)S(1)}, f32[1,8,64,2048]{3,2,1,0:T(8,128)}, u32[]{:S(2)}) copy-start(f32[1,8,64,2048]{3,2,1,0:T(8,128)} %get-tuple-element.292) | copy-start | bytes 12582916 | tf_op jit(solution)/shard_map/while
  102.3 13.2 %copy-start.1 = (f32[1,8,64,2048]{3,2,1,0:T(8,128)S(1)}, f32[1,8,64,2048]{3,2,1,0:T(8,128)}, u32[]{:S(2)}) copy-start(f32[1,8,64,2048]{3,2,1,0:T(8,128)} %get-tuple-element.291) | copy-start | bytes 12582916 | tf_op jit(solution)/shard_map/while
  158.9 14.1 %copy-start = (f32[1,8,64,2048]{3,2,1,0:T(8,128)S(1)}, f32[1,8,64,2048]{3,2,1,0:T(8,128)}, u32[]{:S(2)}) copy-start(f32[1,8,64,2048]{3,2,1,0:T(8,128)} %get-tuple-element.292) | copy-start | bytes 12582916 | tf_op jit(solution)/shard_map/while
  158.9 14.1 %copy-start.1 = (f32[1,8,64,2048]{3,2,1,0:T(8,128)S(1)}, f32[1,8,64,2048]{3,2,1,0:T(8,128)}, u32[]{:S(2)}) copy-start(f32[1,8,64,2048]{3,2,1,0:T(8,128)} %get-tuple-element.291) | copy-start | bytes 12582916 | tf_op jit(solution)/shard_map/while
  216.4 14.5 %copy-start = (f32[1,8,64,2048]{3,2,1,0:T(8,128)S(1)}, f32[1,8,64,2048]{3,2,1,0:T(8,128)}, u32[]{:S(2)}) copy-start(f32[1,8,64,2048]{3,2,1,0:T(8,128)} %get-tuple-element.292) | copy-start | bytes 12582916 | tf_op jit(solution)/shard_map/while
  216.4 14.5 %copy-start.1 = (f32[1,8,64,2048]{3,2,1,0:T(8,128)S(1)}, f32[1,8,64,2048]{3,2,1,0:T(8,128)}, u32[]{:S(2)}) copy-start(f32[1,8,64,2048]{3,2,1,0:T(8,128)} %get-tuple-element.291) | copy-start | bytes 12582916 | tf_op jit(solution)/shard_map/while
  274.1 13.8 %copy-start = (f32[1,8,64,2048]{3,2,1,0:T(8,128)S(1)}, f32[1,8,64,2048]{3,2,1,0:T(8,128)}, u32[]{:S(2)}) copy-start(f32[1,8,64,2048]{3,2,1,0:T(8,128)} %get-tuple-element.292) | copy-start | bytes 12582916 | tf_op jit(solution)/shard_map/while
  274.1 13.8 %copy-start.1 = (f32[1,8,64,2048]{3,2,1,0:T(8,128)S(1)}, f32[1,8,64,2048]{3,2,1,0:T(8,128)}, u32[]{:S(2)}) copy-start(f32[1,8,64,2048]{3,2,1,0:T(8,128)} %get-tuple-element.291) | copy-start | bytes 12582916 | tf_op jit(solution)/shard_map/while
  331.6 14.3 %copy-start = (f32[1,8,64,2048]{3,2,1,0:T(8,128)S(1)}, f32[1,8,64,2048]{3,2,1,0:T(8,128)}, u32[]{:S(2)}) copy-start(f32[1,8,64,2048]{3,2,1,0:T(8,128)} %get-tuple-element.292) | copy-start | bytes 12582916 | tf_op jit(solution)/shard_map/while
  331.6 14.3 %copy-start.1 = (f32[1,8,64,2048]{3,2,1,0:T(8,128)S(1)}, f32[1,8,64,2048]{3,2,1,0:T(8,128)}, u32[]{:S(2)}) copy-start(f32[1,8,64,2048]{3,2,1,0:T(8,128)} %get-tuple-element.291) | copy-start | bytes 12582916 | tf_op jit(solution)/shard_map/while
  389.4 14.0 %copy-start = (f32[1,8,64,2048]{3,2,1,0:T(8,128)S(1)}, f32[1,8,64,2048]{3,2,1,0:T(8,128)}, u32[]{:S(2)}) copy-start(f32[1,8,64,2048]{3,2,1,0:T(8,128)} %get-tuple-element.292) | copy-start | bytes 12582916 | tf_op jit(solution)/shard_map/while
  389.4 14.0 %copy-start.1 = (f32[1,8,64,2048]{3,2,1,0:T(8,128)S(1)}, f32[1,8,64,2048]{3,2,1,0:T(8,128)}, u32[]{:S(2)}) copy-start(f32[1,8,64,2048]{3,2,1,0:T(8,128)} %get-tuple-element.291) | copy-start | bytes 12582916 | tf_op jit(solution)/shard_map/while
  416.5 25.4 %collective-permute-start.4 = (f32[4,64,2,512]{3,2,1,0:T(2,128)S(1)}, f32[4,64,2,512]{3,2,1,0:T(2,128)S(1)}, u32[]{:S(2)}, u32[]{:S(2)}) collective-permute-start(f32[4,64,2,512]{3,2,1,0:T(2,128)S(1)} %bitcast.81), channel_id=1, source_target_pairs={{0,8},{8,0},{16,24},{24,16},{1,9},{9,1},{17,25},{25,17},{2,10},{10... | collective-permute-start | bytes 3145736 | tf_op jit(solution)/shard_map/ppermute | solution.py:27
  446.0 27.4 %collective-permute-start.5 = (f32[4,64,1,512]{3,2,1,0:T(1,128)S(1)}, f32[4,64,1,512]{3,2,1,0:T(1,128)S(1)}, u32[]{:S(2)}, u32[]{:S(2)}) collective-permute-start(f32[4,64,1,512]{3,2,1,0:T(1,128)S(1)} %fusion.8), channel_id=1, source_target_pairs={{0,16},{8,24},{16,0},{24,8},{1,17},{9,25},{17,1},{25,9},{2,18},{10... | collective-permute-start | bytes 1572872 | tf_op jit(solution)/shard_map/ppermute | solution.py:27
where the time goes:
time: 478 us; the launch traced here: 476 us
  other arithmetic  313 us (65%)
  local copies, waits for them, and re-layouts  82.7 us (17%)
  waiting for transfers between devices  60.1 us (13%)
  starting transfers between devices  14.6 us (3%)
    another operation x12, other arithmetic, emit(): jnp.stack([(transfer[channel] + transfer[3 + channel] * tinting) * weight...  171 us
    another operation x6, other arithmetic, march(): before = jnp.cumsum(depth_term, 0) - depth_term  83.7 us
    slice x6, local copies, waits for them, and re-layouts, slope_cols(): right = jnp.concatenate([center[..., 1:], zero_col], -1)  50 us
    ppermute x2, waiting for transfers between devices, partner(): return lax.ppermute(value, axis, pairs)  46.8 us
    reduce_sum x6, other arithmetic, march(): color = color + jnp.sum(passing[None] * emitted, 1)  23.7 us
    concatenate x1, other arithmetic, with_halo(): jnp.concatenate([lax.ppermute(tail, axis, [(i, (i + 1) % count) for i in...  20.7 us
    unnamed x10, local copies, waits for them, and re-layouts  19.2 us
    ppermute x2, waiting for transfers between devices, with_halo(): lax.ppermute(tail, axis, [(i, (i + 1) % count) for i in range(ends)])  9.83 us
  transfers between devices with their start and end apart: 6, of which 4 were waited for; matrix products, arithmetic and copies ran while one was open for 2% of the time, Pallas kernels for 0%

commit v1 on v0

v1 whole, which is shorter than its diff:
```python
import functools
import math

import jax
import jax.numpy as jnp
from jax import lax
from jax.experimental import pallas as pl
from jax.experimental.pallas import tpu as pltpu
from jax.sharding import PartitionSpec as P

LANES = 128
SUBLANES = 8
LN2 = math.log(2.0)


def halo(cells, axis, dim):
    count = lax.axis_size(axis)
    last = cells.shape[dim] - 1
    head = lax.slice_in_dim(cells, 0, 1, axis=dim)
    tail = lax.slice_in_dim(cells, last, last + 1, axis=dim)
    before = lax.ppermute(tail, axis, [(i, i + 1) for i in range(count - 1)])
    after = lax.ppermute(head, axis, [(i + 1, i) for i in range(count - 1)])
    return before, after


def cell(x, below, above, up, down, left, right, state, coef, ends):
    log_t, passing, shade, tinted = state
    gamma, ratio = coef
    first, last = ends
    to_right = pltpu.roll(jnp.where(first, right, x), LANES - 1, 1)
    to_left = pltpu.roll(jnp.where(last, left, x), 1, 1)
    d_col = to_right - to_left
    d_row = down - up
    d_depth = above - below
    plane = d_row + d_col
    along = d_depth + (plane + plane)
    norm = d_depth * d_depth + (d_row * d_row + (d_col * d_col + 4.0))
    lambert = jnp.abs(along) * lax.rsqrt(norm)
    log_t = log_t + gamma * jnp.log2(1.0 + jnp.exp(x))
    after = jnp.exp2(log_t)
    taken = passing - after
    lit = taken * lambert
    shade = shade + lit
    tinted = tinted + (taken + ratio * lit) * jnp.tanh(x)
    return log_t, after, shade, tinted


def spans(slices, parts):
    step = slices // parts
    edges = [0] + [step * (k + 1) + 1 for k in range(parts - 1)] + [slices]
    return [(edges[k], edges[k + 1] - edges[k]) for k in range(parts)]


def render_kernel(
    parts, tiles, block, coef, volume, before, after, above_row, below_row, out, cells, sems, edge_sems
):
    slices, rows, columns = volume.shape
    chunks = out.shape[2] // LANES
    total = columns // LANES
    base = block[0] * chunks
    step = slices // parts
    groups = rows // SUBLANES // tiles
    cuts = spans(slices, parts)
    has_left = base > 0
    has_right = base + chunks < total
    gamma, ratio = coef[0], coef[1]
    lane = lax.broadcasted_iota(jnp.int32, (SUBLANES, LANES), 1)
    ends = (lane == 0, lane == LANES - 1)
    zero = jnp.zeros((SUBLANES, LANES), jnp.float32)
    one = jnp.ones((SUBLANES, LANES), jnp.float32)

    def lanes_of(c):
        at = jnp.clip(base + (c - 1), 0, total - 1)
        return pl.ds(pl.multiple_of(at * LANES, LANES), LANES)

    def body_copy(c, k):
        start, size = cuts[k]
        return pltpu.make_async_copy(
            volume.at[pl.ds(start, size), :, lanes_of(c)],
            cells.at[c, pl.ds(start + 1, size), pl.ds(SUBLANES, rows), :],
            sems.at[c, k],
        )

    def edge_copies(c):
        at = lanes_of(c)
        inner = pl.ds(SUBLANES, rows)
        middle = pl.ds(1, slices)
        return [
            pltpu.make_async_copy(before.at[0, :, at], cells.at[c, 0, inner, :], edge_sems.at[c, 0]),
            pltpu.make_async_copy(
                after.at[0, :, at], cells.at[c, slices + 1, inner, :], edge_sems.at[c, 1]
            ),
            pltpu.make_async_copy(
                above_row.at[:, :, at],
                cells.at[c, middle, pl.ds(SUBLANES - 1, 1), :],
                edge_sems.at[c, 2],
            ),
            pltpu.make_async_copy(
                below_row.at[:, :, at],
                cells.at[c, middle, pl.ds(SUBLANES + rows, 1), :],
                edge_sems.at[c, 3],
            ),
        ]

    def clear(c):
        def slice_of(z, carry):
            for r in range(rows // SUBLANES):
                cells[c, z + 1, pl.ds(SUBLANES * (r + 1), SUBLANES), :] = zero
            return carry

        lax.fori_loop(0, slices, slice_of, 0)

    for copy in edge_copies(1):
        copy.start()
    for k in range(parts):
        body_copy(1, k).start()
        pl.when(has_left)(lambda k=k: body_copy(0, k).start())
        body_copy(2, k).start()
    for c in range(3, chunks + 1):
        for k in range(parts):
            body_copy(c, k).start()
    for k in range(parts):
        pl.when(has_right)(lambda k=k: body_copy(chunks + 1, k).start())
    for c in range(2, chunks + 1):
        for copy in edge_copies(c):
            copy.start()
    pl.when(jnp.logical_not(has_left))(lambda: clear(0))
    pl.when(jnp.logical_not(has_right))(lambda: clear(chunks + 1))

    def land(c, k):
        @pl.when(c == 1)
        def _():
            body_copy(1, k).wait()
            body_copy(2, k).wait()
            pl.when(has_left)(lambda: body_copy(0, k).wait())

        @pl.when(jnp.logical_and(c > 1, jnp.logical_or(c < chunks, has_right)))
        def _():
            body_copy(c + 1, k).wait()

    def group(index, carry):
        c = index // groups + 1
        row = pl.multiple_of((index % groups * tiles + 1) * SUBLANES, SUBLANES)
        fresh = index % groups == 0

        @pl.when(fresh)
        def _():
            land(c, 0)
            for copy in edge_copies(c):
                copy.wait()

        def march(k, carry):
            for part in range(1, parts):
                pl.when(jnp.logical_and(fresh, k == part))(lambda part=part: land(c, part))
            states, belows, centers = carry
            for i in range(step):
                z = k * step + (i + 1)
                marched, aboves = [], []
                for t in range(tiles):
                    at = row + SUBLANES * t
                    here = pl.ds(at, SUBLANES)
                    above = cells[c, z + 1, here, :]
                    marched.append(
                        cell(
                            centers[t],
                            belows[t],
                            above,
                            cells[c, z, pl.ds(at - 1, SUBLANES), :],
                            cells[c, z, pl.ds(at + 1, SUBLANES), :],
                            cells[c - 1, z, here, :],
                            cells[c + 1, z, here, :],
                            states[t],
                            (gamma, ratio),
                            ends,
                        )
                    )
                    aboves.append(above)
                states, belows, centers = marched, centers, aboves
            return states, belows, centers

        def rows_at(z):
            return [cells[c, z, pl.ds(row + SUBLANES * t, SUBLANES), :] for t in range(tiles)]

        carry = ([(zero, one, zero, zero)] * tiles, rows_at(0), rows_at(1))
        states, _, _ = lax.fori_loop(0, parts, march, carry)
        at_lanes = pl.ds(pl.multiple_of((c - 1) * LANES, LANES), LANES)
        for t in range(tiles):
            at_rows = pl.ds(pl.multiple_of(row + SUBLANES * (t - 1), SUBLANES), SUBLANES)
            log_t, _, shade, tinted = states[t]
            for channel, value in enumerate((shade, tinted, log_t)):
                out[channel, at_rows, at_lanes] = value
        return 0

    lax.fori_loop(0, chunks * groups, group, 0)


def render(block, coef, volume, edges, width, tiles=4, parts=4):
    slices, rows, _ = volume.shape
    chunks = width // LANES
    smem = pl.BlockSpec(memory_space=pltpu.SMEM)
    hbm = pl.BlockSpec(memory_space=pl.ANY)
    return pl.pallas_call(
        functools.partial(render_kernel, parts, tiles),
        in_specs=[smem, smem] + [hbm] * 5,
        out_specs=pl.BlockSpec(memory_space=pltpu.VMEM),
        out_shape=jax.ShapeDtypeStruct((3, rows, width), jnp.float32),
        scratch_shapes=[
            pltpu.VMEM((chunks + 2, slices + 2, rows + 2 * SUBLANES, LANES), jnp.float32),
            pltpu.SemaphoreType.DMA((chunks + 2, parts)),
            pltpu.SemaphoreType.DMA((chunks + 1, 4)),
        ],
        compiler_params=pltpu.CompilerParams(vmem_limit_bytes=32 << 20),
        name="render",
    )(block, coef, volume, *edges)


def on_device(volume, transfer):
    local_slices, local_rows, columns = volume.shape
    groups = lax.axis_size("depth")
    mine = lax.axis_index("depth")
    slices = local_slices * groups
    width = columns // groups
    edges = halo(volume, "depth", 0) + halo(volume, "row", 1)
    ambient = 0.5 * transfer[7]
    ratio = (1.0 - ambient) / (3.0 * ambient)
    coef = jnp.stack([-2.0 * transfer[6] / slices, ratio])
    shifts = sorted(range(1, groups), key=lambda s: -min(s, groups - s)) + [0]
    parts = []
    for shift in shifts:
        block = jnp.reshape((mine + shift) % groups, (1,)).astype(jnp.int32)
        part = render(block, coef, volume, edges, width)
        if shift:
            pairs = [(i, (i + shift) % groups) for i in range(groups)]
            part = lax.ppermute(part, "depth", pairs)
        parts.append(part)
    sources = [(mine - shift) % groups for shift in shifts]
    shade = tinted = log_t = 0.0
    for i, part in enumerate(parts):
        ahead = 0.0
        for j, other in enumerate(parts):
            if i != j:
                ahead = ahead + jnp.where(sources[j] < sources[i], other[2], 0.0)
        passing = jnp.exp2(ahead)
        shade = shade + passing * part[0]
        tinted = tinted + passing * part[1]
        log_t = log_t + part[2]
    opacity = -jnp.expm1(LN2 * log_t)
    full = ambient * (opacity + ratio * shade)
    tinted = ambient * tinted
    base = [transfer[c] * full + transfer[3 + c] * (0.5 * (full + tinted)) for c in range(3)]
    return jnp.stack(base + [opacity])


def solution(mesh):
    in_specs = (P("depth", "row", None), P())
    out_specs = P(None, "row", "depth")
    return jax.shard_map(
        on_device, mesh=mesh, in_specs=in_specs, out_specs=out_specs, check_vma=False
    )
```

time: 478 us -> 81.9 us (0.17)
  other arithmetic: 313 us -> 5.27 us
  local copies, waits for them, and re-layouts: 82.7 us -> 7.23 us
  waiting for transfers between devices: 60.1 us -> 5.63 us
  Pallas kernels: 0 us -> 43.2 us
    another operation x19 -> x2, other arithmetic: 255 us -> 0.91 us  [the longest x1 0.84 us: on_device(): return jnp.stack(base + [opacity])]
    ppermute x6 -> x7, waiting for transfers between devices: 60.1 us -> 5.63 us  [the longest x2 3.81 us: halo(): before = lax.ppermute(tail, axis, [(i, i + 1) for i in range(count - 1)])]
    slice x15 -> x3, local copies, waits for them, and re-layouts: 56.7 us -> 7.23 us  [the longest x2 5.61 us: halo(): head = lax.slice_in_dim(cells, 0, 1, axis=dim)]
    pallas_call x0 -> x4, Pallas kernels: none -> 43.2 us  [render(): pl.pallas_call(functools.partial(render_kernel, parts, tiles), in_specs=[...]
    reduce_sum x6 -> x0, other arithmetic: 23.7 us -> none  [march(): color = color + jnp.sum(passing[None] * emitted, 1)]
    concatenate x2 -> x0, other arithmetic: 21.5 us -> none  [the longest x1 20.7 us: with_halo(): jnp.concatenate([lax.ppermute(tail, axis, [(i, (i + 1) % count) for i in...]
    unnamed x10 -> x0, local copies, waits for them, and re-layouts: 19.2 us -> none
    ppermute x6 -> x7, starting transfers between devices: 14.6 us -> 16.3 us  [the longest x2 6.69 us: halo(): before = lax.ppermute(tail, axis, [(i, i + 1) for i in range(count - 1)])]
  transfers between devices with their start and end apart: 6 -> 7, of which waited for: 4 -> 2; matrix products, arithmetic and copies ran while one was open for 2% -> 7% of each run, Pallas kernels for 0% -> 40%
where the time goes in v1:
time: 81.9 us; the launch traced here: 81.5 us
  Pallas kernels  43.2 us (53%)
  starting transfers between devices  16.3 us (20%)
  local copies, waits for them, and re-layouts  7.23 us (9%)
  waiting for transfers between devices  5.63 us (7%)
  other arithmetic  5.27 us (6%)
  between operations  3.87 us (5%)
    pallas_call x4, Pallas kernels, render(): pl.pallas_call(functools.partial(render_kernel, parts, tiles), in_specs=[...  43.2 us
    ppermute x2, starting transfers between devices, halo(): before = lax.ppermute(tail, axis, [(i, i + 1) for i in range(count - 1)])  6.69 us
    ppermute x3, starting transfers between devices, on_device(): part = lax.ppermute(part, 'depth', pairs)  6.13 us
    slice x2, local copies, waits for them, and re-layouts, halo(): head = lax.slice_in_dim(cells, 0, 1, axis=dim)  5.61 us
    ppermute x2, waiting for transfers between devices, halo(): before = lax.ppermute(tail, axis, [(i, i + 1) for i in range(count - 1)])  3.81 us
    ppermute x2, starting transfers between devices, halo(): after = lax.ppermute(head, axis, [(i + 1, i) for i in range(count - 1)])  3.5 us
    add x2, other arithmetic, on_device(): transfer[c] * full + transfer[3 + c] * (0.5 * (full + tinted))  3.28 us
    ppermute x2, waiting for transfers between devices, halo(): after = lax.ppermute(head, axis, [(i + 1, i) for i in range(count - 1)])  1.81 us
  transfers between devices with their start and end apart: 7, of which 2 were waited for; matrix products, arithmetic and copies ran while one was open for 7% of the time, Pallas kernels for 40%

profile of v1, /device:TPU:4, one launch (start us, length us, event | category | flops | bytes accessed | tf_op | source)
XLA Modules:
  0.0 81.5 jit_solution(9601360820107983159)
XLA Ops:
  0.0 1.3 %fusion.14 = (f32[1,64,2048]{2,1,0:T(8,128)S(1)}, f32[1,64,2048]{2,1,0:T(8,128)S(1)}) fusion(f32[48,64,2048]{2,1,0:T(8,128)} %volume.7), kind=kLoop, calls=%fused_computation.30 | loop fusion | bytes 2097152 | tf_op jit(solution)/shard_map/slice | solution.py:19
  1.3 1.3 %collective-permute-start.1 = (f32[1,64,2048]{2,1,0:T(8,128)S(1)}, f32[1,64,2048]{2,1,0:T(8,128)S(1)}, u32[]{:S(2)}, u32[]{:S(2)}) collective-permute-start(f32[1,64,2048]{2,1,0:T(8,128)S(1)} %get-tuple-element.11), channel_id=1, source_target_pairs={{8,0},{16,8},{24,16},{9,1},{17,9},{25,17},{10,2},{18,10},{26,18},{... | collective-permute-start | bytes 1572872 | tf_op jit(solution)/shard_map/ppermute | solution.py:22
  2.6 4.6 %collective-permute-start = (f32[1,64,2048]{2,1,0:T(8,128)S(1)}, f32[1,64,2048]{2,1,0:T(8,128)S(1)}, u32[]{:S(2)}, u32[]{:S(2)}) collective-permute-start(f32[1,64,2048]{2,1,0:T(8,128)S(1)} %get-tuple-element.12), channel_id=1, source_target_pairs={{0,8},{8,16},{16,24},{1,9},{9,17},{17,25},{2,10},{10,18},{18,26},{... | collective-permute-start | bytes 1572872 | tf_op jit(solution)/shard_map/ppermute | solution.py:21
  7.2 4.3 %fusion.13 = (f32[48,1,2048]{2,1,0:T(1,128)}, f32[48,1,2048]{2,1,0:T(1,128)S(1)}) fusion(f32[48,64,2048]{2,1,0:T(8,128)} %volume.7), kind=kLoop, calls=%fused_computation.29 | loop fusion | bytes 1572864 | tf_op jit(solution)/shard_map/slice | solution.py:19
  11.5 2.2 %collective-permute-start.3 = (f32[48,1,2048]{2,1,0:T(1,128)}, f32[48,1,2048]{2,1,0:T(1,128)S(1)}, u32[]{:S(2)}, u32[]{:S(2)}) collective-permute-start(f32[48,1,2048]{2,1,0:T(1,128)} %get-tuple-element.9), channel_id=1, source_target_pairs={{1,0},{2,1},{3,2},{4,3},{5,4},{6,5},{7,6},{9,8},{10,9},{11,10},{12... | collective-permute-start | bytes 1179656 | tf_op jit(solution)/shard_map/ppermute | solution.py:22
  13.7 2.1 %collective-permute-start.2 = (f32[48,1,2048]{2,1,0:T(1,128)S(1)}, f32[48,1,2048]{2,1,0:T(1,128)S(1)}, u32[]{:S(2)}, u32[]{:S(2)}) collective-permute-start(f32[48,1,2048]{2,1,0:T(1,128)S(1)} %get-tuple-element.10), channel_id=1, source_target_pairs={{0,1},{1,2},{2,3},{3,4},{4,5},{5,6},{6,7},{8,9},{9,10},{10,11},{11... | collective-permute-start | bytes 1179656 | tf_op jit(solution)/shard_map/ppermute | solution.py:21
  15.9 1.6 %fusion.15 = (f32[1]{0:T(128)}, f32[1]{0:T(128)}, f32[1]{0:T(128)}, f32[1]{0:T(128)}, f32[1]{0:T(128)}, /*index=5*/f32[1]{0:T(128)}, f32[1]{0:T(128)}, f32[1]{0:T(128)}) fusion(f32[8]{0:T(128)} %param.3), kind=kLoop, calls=%fused_computation.31 | loop fusion | bytes 64 | tf_op jit(solution)/shard_map/slice | solution.py:250
  19.3 0.1 pad_maximum_fusion.1.coef
  19.4 1.8 %collective-permute-done.3.below_row = f32[48,1,2048]{2,1,0:T(1,128)S(1)} collective-permute-done((f32[48,1,2048]{2,1,0:T(1,128)}, f32[48,1,2048]{2,1,0:T(1,128)S(1)}, u32[]{:S(2)}, u32[]{:S(2)}) %collective-permute-start.3) | collective-permute-done | bytes 393248 | tf_op jit(solution)/shard_map/ppermute | solution.py:22
  21.2 3.8 %collective-permute-done.2.above_row = f32[48,1,2048]{2,1,0:T(1,128)S(1)} collective-permute-done((f32[48,1,2048]{2,1,0:T(1,128)S(1)}, f32[48,1,2048]{2,1,0:T(1,128)S(1)}, u32[]{:S(2)}, u32[]{:S(2)}) %collective-permute-start.2) | collective-permute-done | bytes 393248 | tf_op jit(solution)/shard_map/ppermute | solution.py:21
  25.0 0.0 collective-permute-done.1.after
  25.0 0.0 collective-permute-done.before
  25.0 10.9 %render.4 = f32[3,64,512]{2,1,0:T(8,128)S(1)} custom-call(s32[1]{0:T(128)} %bitcast.2.block, f32[2]{0:T(128)S(1)} %pad_maximum_fusion.1.coef, f32[48,64,2048]{2,1,0:T(8,128)} %volume.7, f32[1,64,2048]{2,1,0:T(8,128)S(1)} %collective-permute-done.before, f32[1,64,2048]{2,1,0:T(8,128)S(1)} %collective-permute-done.1.after, ...), custom_call_target="tpu_custom_call" | custom-call | tf_op jit(solution)/shard_map/render/pallas_call | solution.py:202
  35.9 2.2 %collective-permute-start.4 = (f32[3,64,512]{2,1,0:T(8,128)S(1)}, f32[3,64,512]{2,1,0:T(8,128)S(1)}, u32[]{:S(2)}, u32[]{:S(2)}) collective-permute-start(f32[3,64,512]{2,1,0:T(8,128)S(1)} %render.4), channel_id=1, source_target_pairs={{0,16},{8,24},{16,0},{24,8},{1,17},{9,25},{17,1},{25,9},{2,18},{10... | collective-permute-start | bytes 1179656 | tf_op jit(solution)/shard_map/ppermute | solution.py:234
  38.1 10.9 %render.5 = f32[3,64,512]{2,1,0:T(8,128)S(1)} custom-call(s32[1]{0:T(128)} %bitcast.5.block, f32[2]{0:T(128)S(1)} %pad_maximum_fusion.1.coef, f32[48,64,2048]{2,1,0:T(8,128)} %volume.7, f32[1,64,2048]{2,1,0:T(8,128)S(1)} %collective-permute-done.before, f32[1,64,2048]{2,1,0:T(8,128)S(1)} %collective-permute-done.1.after, ...), custom_call_target="tpu_custom_call" | custom-call | tf_op jit(solution)/shard_map/render/pallas_call | solution.py:202
  49.1 0.1 collective-permute-start.5
  49.1 10.9 %render.6 = f32[3,64,512]{2,1,0:T(8,128)S(1)} custom-call(s32[1]{0:T(128)} %bitcast.6.block, f32[2]{0:T(128)S(1)} %pad_maximum_fusion.1.coef, f32[48,64,2048]{2,1,0:T(8,128)} %volume.7, f32[1,64,2048]{2,1,0:T(8,128)S(1)} %collective-permute-done.before, f32[1,64,2048]{2,1,0:T(8,128)S(1)} %collective-permute-done.1.after, ...), custom_call_target="tpu_custom_call" | custom-call | tf_op jit(solution)/shard_map/render/pallas_call | solution.py:202
  60.0 3.9 %collective-permute-start.6 = (f32[3,64,512]{2,1,0:T(8,128)S(1)}, f32[3,64,512]{2,1,0:T(8,128)}, u32[]{:S(2)}, u32[]{:S(2)}) collective-permute-start(f32[3,64,512]{2,1,0:T(8,128)S(1)} %render.6), channel_id=1, source_target_pairs={{0,24},{8,0},{16,8},{24,16},{1,25},{9,1},{17,9},{25,17},{2,26},{10... | collective-permute-start | bytes 1179656 | tf_op jit(solution)/shard_map/ppermute | solution.py:234
  65.8 10.5 %render.7 = f32[3,64,512]{2,1,0:T(8,128)S(1)} custom-call(s32[1]{0:T(128)} %bitcast.7.block, f32[2]{0:T(128)S(1)} %pad_maximum_fusion.1.coef, f32[48,64,2048]{2,1,0:T(8,128)} %volume.7, f32[1,64,2048]{2,1,0:T(8,128)S(1)} %collective-permute-done.before, f32[1,64,2048]{2,1,0:T(8,128)S(1)} %collective-permute-done.1.after, ...), custom_call_target="tpu_custom_call" | custom-call | tf_op jit(solution)/shard_map/render/pallas_call | solution.py:202
  76.3 0.0 collective-permute-done.4
  76.3 0.0 collective-permute-done.5
  76.3 0.0 collective-permute-done.6
  76.3 1.1 %multiply_exponential_fusion.3 = (f32[1,64,512]{2,1,0:T(8,128)S(1)}, f32[1,64,512]{2,1,0:T(8,128)S(1)}, f32[1,64,512]{2,1,0:T(8,128)S(1)}) fusion(f32[3,64,512]{2,1,0:T(8,128)S(1)} %render.7, f32[3,64,512]{2,1,0:T(8,128)} %collective-permute-done.6, f32[3,64,512]{2,1,0:T(8,128)} %collective-permute-done.5, pred[]{:T(512)S(6)} %lt.77, pred[]{:T(512)S(6)} %lt.76, ...), kind=kLoop, calls=%fused_computation.26 | loop fusion | flops 589824 | bytes 917513 | tf_op jit(solution)/shard_map/exp2 | solution.py:243
  77.4 2.1 %multiply_add_fusion.2 = (f32[1,64,512]{2,1,0:T(8,128)S(1)}, f32[1,64,512]{2,1,0:T(8,128)S(1)}, f32[1,64,512]{2,1,0:T(8,128)S(1)}, f32[1,64,512]{2,1,0:T(8,128)S(1)}) fusion(f32[]{:T(128)} %bitcast.8, f32[]{:T(128)} %bitcast, f32[1,64,512]{2,1,0:T(8,128)S(1)} %get-tuple-element.14, f32[3,64,512]{2,1,0:T(8,128)S(1)} %render.7, ...), kind=kLoop, calls=%fused_computation.22 | loop fusion | flops 1081344 | bytes 2490387 | tf_op jit(solution)/shard_map/add | solution.py:250
  79.5 1.1 %multiply_add_fusion.1 = (f32[1,64,512]{2,1,0:T(8,128)S(1)}, f32[1,64,512]{2,1,0:T(8,128)S(1)}) fusion(f32[1,64,512]{2,1,0:T(8,128)S(1)} %get-tuple-element.6, f32[1,64,512]{2,1,0:T(8,128)S(1)} %get-tuple-element.7, f32[]{:T(128)} %bitcast.10, f32[]{:T(128)} %bitcast.9, f32[]{:T(128)} %bitcast.12, f32[]{:T(128)} %bitcast.11), kind=kLoop, calls=%fused_computation.21 | loop fusion | flops 196608 | bytes 524304 | tf_op jit(solution)/shard_map/add | solution.py:250
  80.7 0.8 %pad_maximum_fusion = f32[4,64,512]{2,1,0:T(8,128)} fusion(f32[1,64,512]{2,1,0:T(8,128)S(1)} %get-tuple-element.8, f32[1,64,512]{2,1,0:T(8,128)S(1)} %get-tuple-element.17, f32[1,64,512]{2,1,0:T(8,128)S(1)} %get-tuple-element.16, f32[1,64,512]{2,1,0:T(8,128)S(1)} %get-tuple-element.5), kind=kLoop, calls=%fused_computation | loop fusion | flops 393216 | bytes 1048576 | tf_op jit(solution)/shard_map/stack | solution.py:251
Async XLA Ops:
  1.3 23.7 %collective-permute-start.1 = (f32[1,64,2048]{2,1,0:T(8,128)S(1)}, f32[1,64,2048]{2,1,0:T(8,128)S(1)}, u32[]{:S(2)}, u32[]{:S(2)}) collective-permute-start(f32[1,64,2048]{2,1,0:T(8,128)S(1)} %get-tuple-element.11), channel_id=1, source_target_pairs={{8,0},{16,8},{24,16},{9,1},{17,9},{25,17},{10,2},{18,10},{26,18},{... | collective-permute-start | bytes 1572872 | tf_op jit(solution)/shard_map/ppermute | solution.py:22
  2.6 22.4 %collective-permute-start = (f32[1,64,2048]{2,1,0:T(8,128)S(1)}, f32[1,64,2048]{2,1,0:T(8,128)S(1)}, u32[]{:S(2)}, u32[]{:S(2)}) collective-permute-start(f32[1,64,2048]{2,1,0:T(8,128)S(1)} %get-tuple-element.12), channel_id=1, source_target_pairs={{0,8},{8,16},{16,24},{1,9},{9,17},{17,25},{2,10},{10,18},{18,26},{... | collective-permute-start | bytes 1572872 | tf_op jit(solution)/shard_map/ppermute | solution.py:21
  11.5 9.7 %collective-permute-start.3 = (f32[48,1,2048]{2,1,0:T(1,128)}, f32[48,1,2048]{2,1,0:T(1,128)S(1)}, u32[]{:S(2)}, u32[]{:S(2)}) collective-permute-start(f32[48,1,2048]{2,1,0:T(1,128)} %get-tuple-element.9), channel_id=1, source_target_pairs={{1,0},{2,1},{3,2},{4,3},{5,4},{6,5},{7,6},{9,8},{10,9},{11,10},{12... | collective-permute-start | bytes 1179656 | tf_op jit(solution)/shard_map/ppermute | solution.py:22
  13.7 11.3 %collective-permute-start.2 = (f32[48,1,2048]{2,1,0:T(1,128)S(1)}, f32[48,1,2048]{2,1,0:T(1,128)S(1)}, u32[]{:S(2)}, u32[]{:S(2)}) collective-permute-start(f32[48,1,2048]{2,1,0:T(1,128)S(1)} %get-tuple-element.10), channel_id=1, source_target_pairs={{0,1},{1,2},{2,3},{3,4},{4,5},{5,6},{6,7},{8,9},{9,10},{10,11},{11... | collective-permute-start | bytes 1179656 | tf_op jit(solution)/shard_map/ppermute | solution.py:21
  35.9 40.3 %collective-permute-start.4 = (f32[3,64,512]{2,1,0:T(8,128)S(1)}, f32[3,64,512]{2,1,0:T(8,128)S(1)}, u32[]{:S(2)}, u32[]{:S(2)}) collective-permute-start(f32[3,64,512]{2,1,0:T(8,128)S(1)} %render.4), channel_id=1, source_target_pairs={{0,16},{8,24},{16,0},{24,8},{1,17},{9,25},{17,1},{25,9},{2,18},{10... | collective-permute-start | bytes 1179656 | tf_op jit(solution)/shard_map/ppermute | solution.py:234
  49.1 27.2 %collective-permute-start.5 = (f32[3,64,512]{2,1,0:T(8,128)S(1)}, f32[3,64,512]{2,1,0:T(8,128)}, u32[]{:S(2)}, u32[]{:S(2)}) collective-permute-start(f32[3,64,512]{2,1,0:T(8,128)S(1)} %render.5), channel_id=1, source_target_pairs={{0,8},{8,16},{16,24},{24,0},{1,9},{9,17},{17,25},{25,1},{2,10},{10... | collective-permute-start | bytes 1179656 | tf_op jit(solution)/shard_map/ppermute | solution.py:234
  60.0 16.2 %collective-permute-start.6 = (f32[3,64,512]{2,1,0:T(8,128)S(1)}, f32[3,64,512]{2,1,0:T(8,128)}, u32[]{:S(2)}, u32[]{:S(2)}) collective-permute-start(f32[3,64,512]{2,1,0:T(8,128)S(1)} %render.6), channel_id=1, source_target_pairs={{0,24},{8,0},{16,8},{24,16},{1,25},{9,1},{17,9},{25,17},{2,26},{10... | collective-permute-start | bytes 1179656 | tf_op jit(solution)/shard_map/ppermute | solution.py:234

commit v2 on v0

v2 whole, which is shorter than its diff:
```python
import functools
import math

import jax
import jax.numpy as jnp
from jax import lax
from jax.experimental import pallas as pl
from jax.experimental.pallas import tpu as pltpu
from jax.sharding import PartitionSpec as P

LANES = 128
SUBLANES = 8
LN2 = math.log(2.0)
SMEM = pl.BlockSpec(memory_space=pltpu.SMEM)
VMEM = pl.BlockSpec(memory_space=pltpu.VMEM)
ANY = pl.BlockSpec(memory_space=pl.ANY)


def cut_kernel(volume, first, last, top, bottom, sems):
    slices, rows, _ = volume.shape
    copies = [
        pltpu.make_async_copy(source, target, sems.at[i])
        for i, (source, target) in enumerate(
            [
                (volume.at[pl.ds(0, 1)], first),
                (volume.at[pl.ds(slices - 1, 1)], last),
                (volume.at[:, pl.ds(0, 1), :], top),
                (volume.at[:, pl.ds(rows - 1, 1), :], bottom),
            ]
        )
    ]
    for copy in copies:
        copy.start()
    for copy in copies:
        copy.wait()


def cut(volume):
    slices, rows, columns = volume.shape
    slab = jax.ShapeDtypeStruct((1, rows, columns), jnp.float32)
    strip = jax.ShapeDtypeStruct((slices, 1, columns), jnp.float32)
    return pl.pallas_call(
        cut_kernel,
        in_specs=[ANY],
        out_specs=[ANY] * 4,
        out_shape=[slab, slab, strip, strip],
        scratch_shapes=[pltpu.SemaphoreType.DMA((4,))],
        name="cut",
    )(volume)


def pass_on(value, axis, forward):
    count = lax.axis_size(axis)
    pairs = [(i, i + 1) if forward else (i + 1, i) for i in range(count - 1)]
    return lax.ppermute(value, axis, pairs)


def tile_constants():
    lane = lax.broadcasted_iota(jnp.int32, (SUBLANES, LANES), 1)
    return lane == 0, lane == LANES - 1


def coefficients(transfer, slices):
    gamma = jnp.full((SUBLANES, LANES), transfer[6], jnp.float32) * (-2.0 / slices)
    ambient = 0.5 * jnp.full((SUBLANES, LANES), transfer[7], jnp.float32)
    return gamma, (1.0 - ambient) / (3.0 * ambient)


def cell(cells, c, z, row, x, below, above, state, coef, ends):
    log_t, passing, shade, tinted = state
    gamma, ratio = coef
    first, last = ends
    here = pl.ds(row, SUBLANES)
    right = cells[c + 1, z, here, :]
    left = cells[c - 1, z, here, :]
    d_row = cells[c, z, pl.ds(row + 1, SUBLANES), :] - cells[c, z, pl.ds(row - 1, SUBLANES), :]
    to_right = pltpu.roll(jnp.where(first, right, x), LANES - 1, 1)
    to_left = pltpu.roll(jnp.where(last, left, x), 1, 1)
    d_col = to_right - to_left
    d_depth = above - below
    plane = d_row + d_col
    along = d_depth + (plane + plane)
    norm = d_depth * d_depth + (d_row * d_row + (d_col * d_col + 4.0))
    lambert = jnp.abs(along) * lax.rsqrt(norm)
    log_t = log_t + gamma * jnp.log2(1.0 + jnp.exp(x))
    after = jnp.exp2(log_t)
    taken = passing - after
    lit = taken * lambert
    shade = shade + lit
    tinted = tinted + (taken + ratio * lit) * jnp.tanh(x)
    return log_t, after, shade, tinted


def fresh_state():
    zero = jnp.zeros((SUBLANES, LANES), jnp.float32)
    return zero, jnp.ones((SUBLANES, LANES), jnp.float32), zero, zero


def put(out, c, row, state):
    log_t, _, shade, tinted = state
    rows = pl.ds(row - SUBLANES, SUBLANES)
    lanes = pl.ds((c - 1) * LANES, LANES)
    if not isinstance(row, int):
        rows = pl.ds(pl.multiple_of(row - SUBLANES, SUBLANES), SUBLANES)
    if not isinstance(c, int):
        lanes = pl.ds(pl.multiple_of((c - 1) * LANES, LANES), LANES)
    for channel, value in enumerate((shade, tinted, log_t)):
        out[channel, rows, lanes] = value


class Bricks:
    def __init__(self, volume, cells, sems, shift, chunks, pieces):
        self.volume, self.cells, self.sems, self.pieces = volume, cells, sems, pieces
        self.chunks = chunks
        self.total = volume.shape[2] // LANES
        block = lax.rem(lax.axis_index("depth") + shift, lax.axis_size("depth"))
        self.base = block * chunks
        self.has_left = self.base > 0
        self.has_right = self.base + chunks < self.total

    def lanes(self, c):
        at = jnp.clip(self.base + (c - 1), 0, self.total - 1)
        return pl.ds(pl.multiple_of(at * LANES, LANES), LANES)

    def copy(self, c, k):
        z, depth, y, height = self.pieces[k]
        return pltpu.make_async_copy(
            self.volume.at[pl.ds(z, depth), pl.ds(y, height), self.lanes(c)],
            self.cells.at[c, pl.ds(z + 1, depth), pl.ds(y + SUBLANES, height), :],
            self.sems.at[c, k],
        )

    def clear(self, c):
        slices, rows, _ = self.volume.shape
        zero = jnp.zeros((SUBLANES, LANES), jnp.float32)

        def slice_of(z, carry):
            for r in range(rows // SUBLANES):
                self.cells[c, z + 1, pl.ds(SUBLANES * (r + 1), SUBLANES), :] = zero
            return carry

        lax.fori_loop(0, slices, slice_of, 0)

    def start(self, k, chunks):
        for c in chunks:
            if c == 0:
                pl.when(self.has_left)(lambda: self.copy(0, k).start())
            elif c == self.chunks + 1:
                pl.when(self.has_right)(lambda: self.copy(self.chunks + 1, k).start())
            else:
                self.copy(c, k).start()

    def start_all(self):
        for k in range(len(self.pieces)):
            self.start(k, (1, 0, 2))
        for c in range(3, self.chunks + 2):
            for k in range(len(self.pieces)):
                self.start(k, (c,))
        pl.when(jnp.logical_not(self.has_left))(lambda: self.clear(0))
        pl.when(jnp.logical_not(self.has_right))(lambda: self.clear(self.chunks + 1))

    def land(self, c, k):
        @pl.when(c == 1)
        def _():
            self.copy(1, k).wait()
            self.copy(2, k).wait()
            pl.when(self.has_left)(lambda: self.copy(0, k).wait())

        @pl.when(jnp.logical_and(c > 1, jnp.logical_or(c < self.chunks, self.has_right)))
        def _():
            self.copy(c + 1, k).wait()


def edge_copies(bricks, edges, sems, c):
    before, after, above_row, below_row = edges
    slices, rows, _ = bricks.volume.shape
    cells, at = bricks.cells, bricks.lanes(c)
    inner = pl.ds(SUBLANES, rows)
    middle = pl.ds(1, slices)
    pairs = [
        (before.at[0, :, at], cells.at[c, 0, inner, :]),
        (after.at[0, :, at], cells.at[c, slices + 1, inner, :]),
        (above_row.at[:, :, at], cells.at[c, middle, pl.ds(SUBLANES - 1, 1), :]),
        (below_row.at[:, :, at], cells.at[c, middle, pl.ds(SUBLANES + rows, 1), :]),
    ]
    return [pltpu.make_async_copy(*pair, sems.at[c, i]) for i, pair in enumerate(pairs)]


def march(cells, c, rows, begin, step, trips, coef, ends, arrive):
    def at(z):
        return [cells[c, z, pl.ds(row, SUBLANES), :] for row in rows]

    def trip(k, carry):
        arrive(k)
        states, belows, centers = carry
        for i in range(step):
            z = begin + 1 + k * step + i
            aboves = at(z + 1)
            states = [
                cell(cells, c, z, *tile, coef, ends)
                for tile in zip(rows, centers, belows, aboves, states)
            ]
            belows, centers = centers, aboves
        return states, belows, centers

    carry = ([fresh_state()] * len(rows), at(begin), at(begin + 1))
    if trips == 1:
        return trip(0, carry)[0]
    return lax.fori_loop(0, trips, trip, carry)[0]


def full_kernel(shift, tiles, pieces, total_slices, transfer, volume, *refs):
    *edges, out, cells, sems, edge_sems = refs
    slices, rows, _ = volume.shape
    chunks = out.shape[2] // LANES
    trips = len(pieces)
    groups = rows // SUBLANES // tiles
    bricks = Bricks(volume, cells, sems, shift, chunks, pieces)
    for copy in edge_copies(bricks, edges, edge_sems, 1):
        copy.start()
    bricks.start_all()
    for c in range(2, chunks + 1):
        for copy in edge_copies(bricks, edges, edge_sems, c):
            copy.start()
    coef = coefficients(transfer, total_slices)
    ends = tile_constants()

    def group(index, carry):
        c = index // groups + 1
        row = pl.multiple_of((index % groups * tiles + 1) * SUBLANES, SUBLANES)
        fresh = index % groups == 0

        @pl.when(fresh)
        def _():
            for copy in edge_copies(bricks, edges, edge_sems, c):
                copy.wait()
            bricks.land(c, 0)

        def arrive(k):
            for part in range(1, trips):
                pl.when(jnp.logical_and(fresh, k == part))(lambda part=part: bricks.land(c, part))

        at_rows = [row + SUBLANES * t for t in range(tiles)]
        states = march(cells, c, at_rows, 0, slices // trips, trips, coef, ends, arrive)
        for at_row, state in zip(at_rows, states):
            put(out, c, at_row, state)
        return carry

    lax.fori_loop(0, chunks * groups, group, 0)


def inner_kernel(shift, pieces, total_slices, transfer, volume, out, cells, sems):
    slices, rows, _ = volume.shape
    chunks = out.shape[2] // LANES
    trips = len(pieces)
    bricks = Bricks(volume, cells, sems, shift, chunks, pieces)
    bricks.start_all()
    coef = coefficients(transfer, total_slices)
    ends = tile_constants()
    at_rows = [SUBLANES * (t + 2) for t in range(rows // SUBLANES - 2)]

    def group(index, carry):
        c = index + 1
        bricks.land(c, 0)

        def arrive(k):
            for part in range(1, trips):
                pl.when(k == part)(lambda part=part: bricks.land(c, part))

        states = march(
            cells, c, at_rows, 1, (slices - 2) // trips, trips, coef, ends, arrive
        )
        for at_row, state in zip(at_rows, states):
            put(out, c, at_row, state)
        return carry

    lax.fori_loop(0, chunks, group, 0)


def rest_kernel(shift, pieces, total_slices, transfer, volume, *refs):
    *edges, inner, out, cells, sems, edge_sems = refs
    slices, rows, _ = volume.shape
    chunks = out.shape[2] // LANES
    bricks = Bricks(volume, cells, sems, shift, chunks, pieces)
    for copy in edge_copies(bricks, edges, edge_sems, 1):
        copy.start()
    bricks.start_all()
    for c in range(2, chunks + 1):
        for copy in edge_copies(bricks, edges, edge_sems, c):
            copy.start()
    coef = coefficients(transfer, total_slices)
    ends = tile_constants()

    def group(index, carry):
        c = index + 1
        for copy in edge_copies(bricks, edges, edge_sems, c):
            copy.wait()
        for k in range(len(pieces)):
            bricks.land(c, k)
        outer = [SUBLANES, rows]
        states = march(cells, c, outer, 0, slices, 1, coef, ends, lambda k: None)
        for at_row, state in zip(outer, states):
            put(out, c, at_row, state)
        lanes = pl.ds(pl.multiple_of((c - 1) * LANES, LANES), LANES)
        for t in range(1, rows // SUBLANES - 1):
            row = SUBLANES * (t + 1)
            here = pl.ds(row, SUBLANES)
            sides = []
            for z in (1, slices):
                below, x, above = [cells[c, z + i, here, :] for i in (-1, 0, 1)]
                sides.append(cell(cells, c, z, row, x, below, above, fresh_state(), coef, ends))
            (log_a, pass_a, shade_a, tint_a), (log_b, _, shade_b, tint_b) = sides
            shade, tint, log_t = [inner[i, pl.ds(row - SUBLANES, SUBLANES), lanes] for i in range(3)]
            passing = jnp.exp2(log_t)
            shade = shade_a + pass_a * (shade + passing * shade_b)
            tint = tint_a + pass_a * (tint + passing * tint_b)
            put(out, c, row, (log_a + log_t + log_b, None, shade, tint))
        return carry

    lax.fori_loop(0, chunks, group, 0)


def render(kernel, pieces, name, transfer, volume, extra, width, halo):
    slices, rows, columns = volume.shape
    chunks = width // LANES
    scratch = [
        pltpu.VMEM((chunks + 2, slices + 2, rows + 2 * SUBLANES, LANES), jnp.float32),
        pltpu.SemaphoreType.DMA((chunks + 2, len(pieces))),
    ]
    if halo:
        scratch.append(pltpu.SemaphoreType.DMA((chunks + 1, 4)))
    return pl.pallas_call(
        kernel,
        in_specs=[SMEM, ANY] + [ANY] * min(4, len(extra)) + [VMEM] * (len(extra) - 4),
        out_specs=VMEM,
        out_shape=jax.ShapeDtypeStruct((3, rows, width), jnp.float32),
        scratch_shapes=scratch,
        compiler_params=pltpu.CompilerParams(vmem_limit_bytes=32 << 20),
        name=name,
    )(transfer, volume, *extra)


def merge_kernel(shifts, transfer, *refs):
    *parts, out = refs
    count = len(parts)
    mine = lax.axis_index("depth")
    rows, width = out.shape[1:]
    sources = [lax.rem(mine - shift + count, count) for shift in shifts]
    nearer = [
        [jnp.where(sources[j] < sources[i], 1.0, 0.0) for j in range(count)] for i in range(count)
    ]
    ambient = 0.5 * jnp.full((SUBLANES, LANES), transfer[7], jnp.float32)
    spread = (1.0 - ambient) / 3.0

    def band(r, carry):
        here = pl.ds(pl.multiple_of(r * SUBLANES, SUBLANES), SUBLANES)
        for x in range(width // LANES):
            at = pl.ds(x * LANES, LANES)
            shade = tinted = log_t = jnp.zeros((SUBLANES, LANES), jnp.float32)
            logs = [part[2, here, at] for part in parts]
            for i, part in enumerate(parts):
                ahead = sum(logs[j] * nearer[i][j] for j in range(count) if j != i)
                passing = jnp.exp2(ahead)
                shade = shade + passing * part[0, here, at]
                tinted = tinted + passing * part[1, here, at]
                log_t = log_t + logs[i]
            half = jnp.tanh(log_t * (-0.5 * LN2))
            opacity = (half + half) / (1.0 + half)
            full = ambient * opacity + spread * shade
            mixed = 0.5 * (full + ambient * tinted)
            for color in range(3):
                out[color, here, at] = transfer[color] * full + transfer[3 + color] * mixed
            out[3, here, at] = opacity
        return carry

    lax.fori_loop(0, rows // SUBLANES, band, 0)


def merge(parts, shifts, transfer):
    _, rows, width = parts[0].shape
    return pl.pallas_call(
        functools.partial(merge_kernel, shifts),
        in_specs=[SMEM] + [VMEM] * len(parts),
        out_specs=VMEM,
        out_shape=jax.ShapeDtypeStruct((4, rows, width), jnp.float32),
        compiler_params=pltpu.CompilerParams(vmem_limit_bytes=16 << 20),
        name="merge",
    )(transfer, *parts)


def on_device(volume, transfer):
    slices, rows, columns = volume.shape
    groups = lax.axis_size("depth")
    total_slices = slices * groups
    width = columns // groups
    first, last, top, bottom = cut(volume)
    edges = (
        pass_on(last, "depth", True),
        pass_on(first, "depth", False),
        pass_on(bottom, "row", True),
        pass_on(top, "row", False),
    )
    half = slices // 2
    halves = [(0, half + 1, 0, rows), (half + 1, slices - half - 1, 0, rows)]
    ring = [
        (0, slices, 0, 2 * SUBLANES),
        (0, slices, rows - 2 * SUBLANES, 2 * SUBLANES),
        (0, 2, 2 * SUBLANES, rows - 4 * SUBLANES),
        (slices - 2, 2, 2 * SUBLANES, rows - 4 * SUBLANES),
    ]
    shifts = sorted(range(1, groups), key=lambda s: -min(s, groups - s)) + [0]
    parts = []
    for shift in shifts:
        if not parts:
            kernel = functools.partial(inner_kernel, shift, halves, total_slices)
            inner = render(kernel, halves, "inner", transfer, volume, (), width, False)
            kernel = functools.partial(rest_kernel, shift, ring, total_slices)
            part = render(kernel, ring, "rest", transfer, volume, edges + (inner,), width, True)
        else:
            kernel = functools.partial(full_kernel, shift, 8, halves, total_slices)
            part = render(kernel, halves, "full", transfer, volume, edges, width, True)
        if shift:
            pairs = [(i, (i + shift) % groups) for i in range(groups)]
            part = lax.ppermute(part, "depth", pairs)
        parts.append(part)
    return merge(parts, shifts, transfer)


def solution(mesh):
    in_specs = (P("depth", "row", None), P())
    out_specs = P(None, "row", "depth")
    return jax.shard_map(
        on_device, mesh=mesh, in_specs=in_specs, out_specs=out_specs, check_vma=False
    )
```

time: 478 us -> 129 us (0.27)
  the two profiles are of different devices: /device:TPU:4 before, /device:TPU:0 now
where the time goes in v2:
time: 129 us
  Pallas kernels  99.1 us (77%)
  waiting for transfers between devices  16.7 us (13%)
  starting transfers between devices  13.3 us (10%)
    pallas_call x1, Pallas kernels, cut(): pl.pallas_call(cut_kernel, in_specs=[ANY], out_specs=[ANY] * 4, out_shape...  56.7 us
    pallas_call x5, Pallas kernels, render(): pl.pallas_call(kernel, in_specs=[SMEM, ANY] + [ANY] * min(4, len(extra))...  40.6 us
    ppermute x3, waiting for transfers between devices, on_device(): part = lax.ppermute(part, 'depth', pairs)  13 us
    ppermute x4, starting transfers between devices, pass_on(): return lax.ppermute(value, axis, pairs)  9.06 us
    ppermute x3, starting transfers between devices, on_device(): part = lax.ppermute(part, 'depth', pairs)  4.24 us
    ppermute x4, waiting for transfers between devices, pass_on(): return lax.ppermute(value, axis, pairs)  3.7 us
  transfers between devices with their start and end apart: 7, of which 2 were waited for; matrix products, arithmetic and copies ran while one was open for 0% of the time, Pallas kernels for 24%

profile of v2, /device:TPU:0, one launch (start us, length us, event | category | flops | bytes accessed | tf_op | source)
XLA Modules:
  0.0 129.2 jit_solution(421322007535372618)
XLA Ops:
  0.0 0.0 copy-start
  0.0 56.7 %cut.1 = (f32[1,64,2048]{2,1,0:T(8,128)}, f32[1,64,2048]{2,1,0:T(8,128)}, f32[48,1,2048]{2,1,0:T(1,128)}, f32[48,1,2048]{2,1,0:T(1,128)}) custom-call(f32[48,64,2048]{2,1,0:T(8,128)} %volume.11), custom_call_target="tpu_custom_call" | custom-call | tf_op jit(solution)/shard_map/cut/pallas_call | solution.py:42
  56.7 5.0 %collective-permute-start = (f32[1,64,2048]{2,1,0:T(8,128)}, f32[1,64,2048]{2,1,0:T(8,128)S(1)}, u32[]{:S(2)}, u32[]{:S(2)}) collective-permute-start(f32[1,64,2048]{2,1,0:T(8,128)} %get-tuple-element.9), channel_id=1, source_target_pairs={{0,8},{8,16},{16,24},{1,9},{9,17},{17,25},{2,10},{10,18},{18,26},{... | collective-permute-start | bytes 1572872 | tf_op jit(solution)/shard_map/ppermute | solution.py:55
  61.7 1.3 collective-permute-start.1
  63.0 1.5 %collective-permute-start.2 = (f32[48,1,2048]{2,1,0:T(1,128)}, f32[48,1,2048]{2,1,0:T(1,128)S(1)}, u32[]{:S(2)}, u32[]{:S(2)}) collective-permute-start(f32[48,1,2048]{2,1,0:T(1,128)} %get-tuple-element.11), channel_id=1, source_target_pairs={{0,1},{1,2},{2,3},{3,4},{4,5},{5,6},{6,7},{8,9},{9,10},{10,11},{11... | collective-permute-start | bytes 1179656 | tf_op jit(solution)/shard_map/ppermute | solution.py:55
  64.5 1.3 collective-permute-start.3
  65.8 0.0 copy-done
  65.8 7.7 %inner.1.refs_4_ = f32[3,64,512]{2,1,0:T(8,128)S(1)} custom-call(f32[8]{0:T(128)S(1)} %copy-done, f32[48,64,2048]{2,1,0:T(8,128)} %volume.11), custom_call_target="tpu_custom_call" | custom-call | tf_op jit(solution)/shard_map/inner/pallas_call | solution.py:332
  73.5 0.0 collective-permute-done.2.refs_2_
  73.5 0.0 collective-permute-done.3.refs_3_
  73.5 0.0 collective-permute-done.refs_0_
  73.5 3.7 %collective-permute-done.1.refs_1_ = f32[1,64,2048]{2,1,0:T(8,128)S(1)} collective-permute-done((f32[1,64,2048]{2,1,0:T(8,128)}, f32[1,64,2048]{2,1,0:T(8,128)S(1)}, u32[]{:S(2)}, u32[]{:S(2)}) %collective-permute-start.1) | collective-permute-done | bytes 524320 | tf_op jit(solution)/shard_map/ppermute | solution.py:55
  77.2 9.5 %full.3 = f32[3,64,512]{2,1,0:T(8,128)S(1)} custom-call(f32[8]{0:T(128)S(1)} %copy-done, f32[48,64,2048]{2,1,0:T(8,128)} %volume.11, f32[1,64,2048]{2,1,0:T(8,128)S(1)} %collective-permute-done.refs_0_, f32[1,64,2048]{2,1,0:T(8,128)S(1)} %collective-permute-done.1.refs_1_, f32[48,1,2048]{2,1,0:T(1,128)S(1)} %collective-permute-done.2.refs_2_, ...), custom_call_target="tpu_custom_call" | custom-call | tf_op jit(solution)/shard_map/full/pallas_call | solution.py:332
  86.8 1.6 %collective-permute-start.5 = (f32[3,64,512]{2,1,0:T(8,128)S(1)}, f32[3,64,512]{2,1,0:T(8,128)S(1)}, u32[]{:S(2)}, u32[]{:S(2)}) collective-permute-start(f32[3,64,512]{2,1,0:T(8,128)S(1)} %full.3), channel_id=1, source_target_pairs={{0,8},{8,16},{16,24},{24,0},{1,9},{9,17},{17,25},{25,1},{2,10},{10... | collective-permute-start | bytes 1179656 | tf_op jit(solution)/shard_map/ppermute | solution.py:424
  88.4 9.5 %full.4 = f32[3,64,512]{2,1,0:T(8,128)S(1)} custom-call(f32[8]{0:T(128)S(1)} %copy-done, f32[48,64,2048]{2,1,0:T(8,128)} %volume.11, f32[1,64,2048]{2,1,0:T(8,128)S(1)} %collective-permute-done.refs_0_, f32[1,64,2048]{2,1,0:T(8,128)S(1)} %collective-permute-done.1.refs_1_, f32[48,1,2048]{2,1,0:T(1,128)S(1)} %collective-permute-done.2.refs_2_, ...), custom_call_target="tpu_custom_call" | custom-call | tf_op jit(solution)/shard_map/full/pallas_call | solution.py:332
  97.9 2.3 %collective-permute-start.6 = (f32[3,64,512]{2,1,0:T(8,128)S(1)}, f32[3,64,512]{2,1,0:T(8,128)S(1)}, u32[]{:S(2)}, u32[]{:S(2)}) collective-permute-start(f32[3,64,512]{2,1,0:T(8,128)S(1)} %full.4), channel_id=1, source_target_pairs={{0,24},{8,0},{16,8},{24,16},{1,25},{9,1},{17,9},{25,17},{2,26},{10... | collective-permute-start | bytes 1179656 | tf_op jit(solution)/shard_map/ppermute | solution.py:424
  100.2 4.7 %rest.1 = f32[3,64,512]{2,1,0:T(8,128)S(1)} custom-call(f32[8]{0:T(128)S(1)} %copy-done, f32[48,64,2048]{2,1,0:T(8,128)} %volume.11, f32[1,64,2048]{2,1,0:T(8,128)S(1)} %collective-permute-done.refs_0_, f32[1,64,2048]{2,1,0:T(8,128)S(1)} %collective-permute-done.1.refs_1_, f32[48,1,2048]{2,1,0:T(1,128)S(1)} %collective-permute-done.2.refs_2_, ...), custom_call_target="tpu_custom_call" | custom-call | tf_op jit(solution)/shard_map/rest/pallas_call | solution.py:332
  104.9 0.3 collective-permute-start.4
  105.2 9.3 %full.5.refs_3_ = f32[3,64,512]{2,1,0:T(8,128)S(1)} custom-call(f32[8]{0:T(128)S(1)} %copy-done, f32[48,64,2048]{2,1,0:T(8,128)} %volume.11, f32[1,64,2048]{2,1,0:T(8,128)S(1)} %collective-permute-done.refs_0_, f32[1,64,2048]{2,1,0:T(8,128)S(1)} %collective-permute-done.1.refs_1_, f32[48,1,2048]{2,1,0:T(1,128)S(1)} %collective-permute-done.2.refs_2_, ...), custom_call_target="tpu_custom_call" | custom-call | tf_op jit(solution)/shard_map/full/pallas_call | solution.py:332
  114.5 0.0 collective-permute-done.5.refs_1_
  114.5 0.0 collective-permute-done.6.refs_2_
  114.5 13.0 %collective-permute-done.4.refs_0_ = f32[3,64,512]{2,1,0:T(8,128)S(1)} collective-permute-done((f32[3,64,512]{2,1,0:T(8,128)S(1)}, f32[3,64,512]{2,1,0:T(8,128)S(1)}, u32[]{:S(2)}, u32[]{:S(2)}) %collective-permute-start.4) | collective-permute-done | bytes 393248 | tf_op jit(solution)/shard_map/ppermute | solution.py:424
  127.5 1.8 %merge.1 = f32[4,64,512]{2,1,0:T(8,128)} custom-call(f32[8]{0:T(128)S(1)} %copy-done, f32[3,64,512]{2,1,0:T(8,128)S(1)} %collective-permute-done.4.refs_0_, f32[3,64,512]{2,1,0:T(8,128)S(1)} %collective-permute-done.5.refs_1_, f32[3,64,512]{2,1,0:T(8,128)S(1)} %collective-permute-done.6.refs_2_, f32[3,64,512]{2,1,0:T(8,128)S(1)} %full.5.refs_3_), custom_call_target="tpu_custom_call" | custom-call | tf_op jit(solution)/shard_map/merge/pallas_call | solution.py:381
Async XLA Ops:
  0.0 65.8 %copy-start = (f32[8]{0:T(128)S(1)}, f32[8]{0:T(128)}, u32[]{:S(2)}) copy-start(f32[8]{0:T(128)} %transfer.11) | copy-start | bytes 100
  56.7 16.8 %collective-permute-start = (f32[1,64,2048]{2,1,0:T(8,128)}, f32[1,64,2048]{2,1,0:T(8,128)S(1)}, u32[]{:S(2)}, u32[]{:S(2)}) collective-permute-start(f32[1,64,2048]{2,1,0:T(8,128)} %get-tuple-element.9), channel_id=1, source_target_pairs={{0,8},{8,16},{16,24},{1,9},{9,17},{17,25},{2,10},{10,18},{18,26},{... | collective-permute-start | bytes 1572872 | tf_op jit(solution)/shard_map/ppermute | solution.py:55
  61.7 15.5 %collective-permute-start.1 = (f32[1,64,2048]{2,1,0:T(8,128)}, f32[1,64,2048]{2,1,0:T(8,128)S(1)}, u32[]{:S(2)}, u32[]{:S(2)}) collective-permute-start(f32[1,64,2048]{2,1,0:T(8,128)} %get-tuple-element.10), channel_id=1, source_target_pairs={{8,0},{16,8},{24,16},{9,1},{17,9},{25,17},{10,2},{18,10},{26,18},{... | collective-permute-start | bytes 1572872 | tf_op jit(solution)/shard_map/ppermute | solution.py:55
  63.0 10.5 %collective-permute-start.2 = (f32[48,1,2048]{2,1,0:T(1,128)}, f32[48,1,2048]{2,1,0:T(1,128)S(1)}, u32[]{:S(2)}, u32[]{:S(2)}) collective-permute-start(f32[48,1,2048]{2,1,0:T(1,128)} %get-tuple-element.11), channel_id=1, source_target_pairs={{0,1},{1,2},{2,3},{3,4},{4,5},{5,6},{6,7},{8,9},{9,10},{10,11},{11... | collective-permute-start | bytes 1179656 | tf_op jit(solution)/shard_map/ppermute | solution.py:55
  64.5 9.0 %collective-permute-start.3 = (f32[48,1,2048]{2,1,0:T(1,128)}, f32[48,1,2048]{2,1,0:T(1,128)S(1)}, u32[]{:S(2)}, u32[]{:S(2)}) collective-permute-start(f32[48,1,2048]{2,1,0:T(1,128)} %get-tuple-element.12), channel_id=1, source_target_pairs={{1,0},{2,1},{3,2},{4,3},{5,4},{6,5},{7,6},{9,8},{10,9},{11,10},{12... | collective-permute-start | bytes 1179656 | tf_op jit(solution)/shard_map/ppermute | solution.py:55
  86.8 27.7 %collective-permute-start.5 = (f32[3,64,512]{2,1,0:T(8,128)S(1)}, f32[3,64,512]{2,1,0:T(8,128)S(1)}, u32[]{:S(2)}, u32[]{:S(2)}) collective-permute-start(f32[3,64,512]{2,1,0:T(8,128)S(1)} %full.3), channel_id=1, source_target_pairs={{0,8},{8,16},{16,24},{24,0},{1,9},{9,17},{17,25},{25,1},{2,10},{10... | collective-permute-start | bytes 1179656 | tf_op jit(solution)/shard_map/ppermute | solution.py:424
  97.9 16.6 %collective-permute-start.6 = (f32[3,64,512]{2,1,0:T(8,128)S(1)}, f32[3,64,512]{2,1,0:T(8,128)S(1)}, u32[]{:S(2)}, u32[]{:S(2)}) collective-permute-start(f32[3,64,512]{2,1,0:T(8,128)S(1)} %full.4), channel_id=1, source_target_pairs={{0,24},{8,0},{16,8},{24,16},{1,25},{9,1},{17,9},{25,17},{2,26},{10... | collective-permute-start | bytes 1179656 | tf_op jit(solution)/shard_map/ppermute | solution.py:424
  104.9 22.6 %collective-permute-start.4 = (f32[3,64,512]{2,1,0:T(8,128)S(1)}, f32[3,64,512]{2,1,0:T(8,128)S(1)}, u32[]{:S(2)}, u32[]{:S(2)}) collective-permute-start(f32[3,64,512]{2,1,0:T(8,128)S(1)} %rest.1), channel_id=1, source_target_pairs={{0,16},{8,24},{16,0},{24,8},{1,17},{9,25},{17,1},{25,9},{2,18},{10... | collective-permute-start | bytes 1179656 | tf_op jit(solution)/shard_map/ppermute | solution.py:424

commit v3 on v2

--- a/solution.py
+++ b/solution.py
@@ -7,6 +7,7 @@
 from jax.experimental import pallas as pl
 from jax.experimental.pallas import tpu as pltpu
 from jax.sharding import PartitionSpec as P
+
 
 LANES = 128
 SUBLANES = 8
@@ -42,7 +43,7 @@
     return pl.pallas_call(
         cut_kernel,
         in_specs=[ANY],
-        out_specs=[ANY] * 4,
+        out_specs=[VMEM] * 4,
         out_shape=[slab, slab, strip, strip],
         scratch_shapes=[pltpu.SemaphoreType.DMA((4,))],
         name="cut",
@@ -320,8 +321,8 @@
     lax.fori_loop(0, chunks, group, 0)
 
 
-def render(kernel, pieces, name, transfer, volume, extra, width, halo):
-    slices, rows, columns = volume.shape
+def render(kernel, pieces, transfer, volume, extra, width, halo):
+    slices, rows, _ = volume.shape
     chunks = width // LANES
     scratch = [
         pltpu.VMEM((chunks + 2, slices + 2, rows + 2 * SUBLANES, LANES), jnp.float32),
@@ -336,7 +337,6 @@
         out_shape=jax.ShapeDtypeStruct((3, rows, width), jnp.float32),
         scratch_shapes=scratch,
         compiler_params=pltpu.CompilerParams(vmem_limit_bytes=32 << 20),
-        name=name,
     )(transfer, volume, *extra)
 
 
@@ -408,17 +408,17 @@
         (0, 2, 2 * SUBLANES, rows - 4 * SUBLANES),
         (slices - 2, 2, 2 * SUBLANES, rows - 4 * SUBLANES),
     ]
-    shifts = sorted(range(1, groups), key=lambda s: -min(s, groups - s)) + [0]
+    shifts = order_of_shifts(groups)
     parts = []
-    for shift in shifts:
-        if not parts:
+    for stage, shift in enumerate(shifts):
+        if stage == 0:
             kernel = functools.partial(inner_kernel, shift, halves, total_slices)
-            inner = render(kernel, halves, "inner", transfer, volume, (), width, False)
+            inner = render(kernel, halves, transfer, volume, (), width, False)
             kernel = functools.partial(rest_kernel, shift, ring, total_slices)
-            part = render(kernel, ring, "rest", transfer, volume, edges + (inner,), width, True)
+            part = render(kernel, ring, transfer, volume, edges + (inner,), width, True)
         else:
             kernel = functools.partial(full_kernel, shift, 8, halves, total_slices)
-            part = render(kernel, halves, "full", transfer, volume, edges, width, True)
+            part = render(kernel, halves, transfer, volume, edges, width, True)
         if shift:
             pairs = [(i, (i + shift) % groups) for i in range(groups)]
             part = lax.ppermute(part, "depth", pairs)
@@ -426,9 +426,14 @@
     return merge(parts, shifts, transfer)
 
 
+def order_of_shifts(groups):
+    return sorted(range(1, groups), key=lambda s: -min(s, groups - s)) + [0]
+
+
 def solution(mesh):
     in_specs = (P("depth", "row", None), P())
     out_specs = P(None, "row", "depth")
+
     return jax.shard_map(
         on_device, mesh=mesh, in_specs=in_specs, out_specs=out_specs, check_vma=False
     )

time: 129 us -> 75.4 us (0.58)
  Pallas kernels: 99.1 us -> 45.1 us
    pallas_call x1, Pallas kernels: 56.7 us -> 2.72 us  [cut(): pl.pallas_call(cut_kernel, in_specs=[ANY], out_specs=[VMEM] * 4, out_shap...]
  transfers between devices with their start and end apart: 7 -> 7, of which waited for: 2 -> 2; matrix products, arithmetic and copies ran while one was open for 0% -> 0% of each run, Pallas kernels for 24% -> 41%
where the time goes in v3:
time: 75.4 us; the launch traced here: 75.2 us
  Pallas kernels  45.1 us (60%)
  waiting for transfers between devices  16.7 us (22%)
  starting transfers between devices  13.3 us (18%)
    pallas_call x5, Pallas kernels, render(): pl.pallas_call(kernel, in_specs=[SMEM, ANY] + [ANY] * min(4, len(extra))...  40.6 us
    ppermute x3, waiting for transfers between devices, on_device(): part = lax.ppermute(part, 'depth', pairs)  13 us
    ppermute x4, starting transfers between devices, pass_on(): return lax.ppermute(value, axis, pairs)  9.06 us
    ppermute x3, starting transfers between devices, on_device(): part = lax.ppermute(part, 'depth', pairs)  4.24 us
    ppermute x4, waiting for transfers between devices, pass_on(): return lax.ppermute(value, axis, pairs)  3.7 us
    pallas_call x1, Pallas kernels, cut(): pl.pallas_call(cut_kernel, in_specs=[ANY], out_specs=[VMEM] * 4, out_shap...  2.72 us
    pallas_call x1, Pallas kernels, merge(): pl.pallas_call(functools.partial(merge_kernel, shifts), in_specs=[SMEM] +...  1.75 us
  transfers between devices with their start and end apart: 7, of which 2 were waited for; matrix products, arithmetic and copies ran while one was open for 0% of the time, Pallas kernels for 41%

profile of v3, /device:TPU:0, one launch (start us, length us, event | category | flops | bytes accessed | tf_op | source)
XLA Modules:
  0.0 75.2 jit_solution(1789281636712305205)
XLA Ops:
  0.0 0.0 copy-start
  0.0 2.7 %cut.1 = (f32[1,64,2048]{2,1,0:T(8,128)}, f32[1,64,2048]{2,1,0:T(8,128)}, f32[48,1,2048]{2,1,0:T(1,128)}, f32[48,1,2048]{2,1,0:T(1,128)}) custom-call(f32[48,64,2048]{2,1,0:T(8,128)} %volume.11), custom_call_target="tpu_custom_call" | custom-call | tf_op jit(solution)/shard_map/cut/pallas_call | solution.py:43
  2.7 5.0 %collective-permute-start = (f32[1,64,2048]{2,1,0:T(8,128)}, f32[1,64,2048]{2,1,0:T(8,128)S(1)}, u32[]{:S(2)}, u32[]{:S(2)}) collective-permute-start(f32[1,64,2048]{2,1,0:T(8,128)} %get-tuple-element.9), channel_id=1, source_target_pairs={{0,8},{8,16},{16,24},{1,9},{9,17},{17,25},{2,10},{10,18},{18,26},{... | collective-permute-start | bytes 1572872 | tf_op jit(solution)/shard_map/ppermute | solution.py:56
  7.7 1.3 %collective-permute-start.1 = (f32[1,64,2048]{2,1,0:T(8,128)}, f32[1,64,2048]{2,1,0:T(8,128)S(1)}, u32[]{:S(2)}, u32[]{:S(2)}) collective-permute-start(f32[1,64,2048]{2,1,0:T(8,128)} %get-tuple-element.10), channel_id=1, source_target_pairs={{8,0},{16,8},{24,16},{9,1},{17,9},{25,17},{10,2},{18,10},{26,18},{... | collective-permute-start | bytes 1572872 | tf_op jit(solution)/shard_map/ppermute | solution.py:56
  9.0 1.5 %collective-permute-start.2 = (f32[48,1,2048]{2,1,0:T(1,128)}, f32[48,1,2048]{2,1,0:T(1,128)S(1)}, u32[]{:S(2)}, u32[]{:S(2)}) collective-permute-start(f32[48,1,2048]{2,1,0:T(1,128)} %get-tuple-element.11), channel_id=1, source_target_pairs={{0,1},{1,2},{2,3},{3,4},{4,5},{5,6},{6,7},{8,9},{9,10},{10,11},{11... | collective-permute-start | bytes 1179656 | tf_op jit(solution)/shard_map/ppermute | solution.py:56
  10.5 1.3 %collective-permute-start.3 = (f32[48,1,2048]{2,1,0:T(1,128)}, f32[48,1,2048]{2,1,0:T(1,128)S(1)}, u32[]{:S(2)}, u32[]{:S(2)}) collective-permute-start(f32[48,1,2048]{2,1,0:T(1,128)} %get-tuple-element.12), channel_id=1, source_target_pairs={{1,0},{2,1},{3,2},{4,3},{5,4},{6,5},{7,6},{9,8},{10,9},{11,10},{12... | collective-permute-start | bytes 1179656 | tf_op jit(solution)/shard_map/ppermute | solution.py:56
  11.8 0.0 copy-done
  11.8 7.7 %shard_map.28.refs_4_ = f32[3,64,512]{2,1,0:T(8,128)S(1)} custom-call(f32[8]{0:T(128)S(1)} %copy-done, f32[48,64,2048]{2,1,0:T(8,128)} %volume.11), custom_call_target="tpu_custom_call" | custom-call | tf_op jit(solution)/shard_map/pallas_call | solution.py:333
  19.5 0.0 collective-permute-done.2.refs_2_
  19.5 0.0 collective-permute-done.3.refs_3_
  19.5 0.0 collective-permute-done.refs_0_
  19.5 3.7 %collective-permute-done.1.refs_1_ = f32[1,64,2048]{2,1,0:T(8,128)S(1)} collective-permute-done((f32[1,64,2048]{2,1,0:T(8,128)}, f32[1,64,2048]{2,1,0:T(8,128)S(1)}, u32[]{:S(2)}, u32[]{:S(2)}) %collective-permute-start.1) | collective-permute-done | bytes 524320 | tf_op jit(solution)/shard_map/ppermute | solution.py:56
  23.2 9.5 %shard_map.30 = f32[3,64,512]{2,1,0:T(8,128)S(1)} custom-call(f32[8]{0:T(128)S(1)} %copy-done, f32[48,64,2048]{2,1,0:T(8,128)} %volume.11, f32[1,64,2048]{2,1,0:T(8,128)S(1)} %collective-permute-done.refs_0_, f32[1,64,2048]{2,1,0:T(8,128)S(1)} %collective-permute-done.1.refs_1_, f32[48,1,2048]{2,1,0:T(1,128)S(1)} %collective-permute-done.2.refs_2_, ...), custom_call_target="tpu_custom_call" | custom-call | tf_op jit(solution)/shard_map/pallas_call | solution.py:333
  32.8 1.6 %collective-permute-start.5 = (f32[3,64,512]{2,1,0:T(8,128)S(1)}, f32[3,64,512]{2,1,0:T(8,128)S(1)}, u32[]{:S(2)}, u32[]{:S(2)}) collective-permute-start(f32[3,64,512]{2,1,0:T(8,128)S(1)} %shard_map.30), channel_id=1, source_target_pairs={{0,8},{8,16},{16,24},{24,0},{1,9},{9,17},{17,25},{25,1},{2,10},{10... | collective-permute-start | bytes 1179656 | tf_op jit(solution)/shard_map/ppermute | solution.py:424
  34.4 9.5 %shard_map.31 = f32[3,64,512]{2,1,0:T(8,128)S(1)} custom-call(f32[8]{0:T(128)S(1)} %copy-done, f32[48,64,2048]{2,1,0:T(8,128)} %volume.11, f32[1,64,2048]{2,1,0:T(8,128)S(1)} %collective-permute-done.refs_0_, f32[1,64,2048]{2,1,0:T(8,128)S(1)} %collective-permute-done.1.refs_1_, f32[48,1,2048]{2,1,0:T(1,128)S(1)} %collective-permute-done.2.refs_2_, ...), custom_call_target="tpu_custom_call" | custom-call | tf_op jit(solution)/shard_map/pallas_call | solution.py:333
  43.9 2.3 %collective-permute-start.6 = (f32[3,64,512]{2,1,0:T(8,128)S(1)}, f32[3,64,512]{2,1,0:T(8,128)S(1)}, u32[]{:S(2)}, u32[]{:S(2)}) collective-permute-start(f32[3,64,512]{2,1,0:T(8,128)S(1)} %shard_map.31), channel_id=1, source_target_pairs={{0,24},{8,0},{16,8},{24,16},{1,25},{9,1},{17,9},{25,17},{2,26},{10... | collective-permute-start | bytes 1179656 | tf_op jit(solution)/shard_map/ppermute | solution.py:424
  46.2 4.7 %shard_map.29 = f32[3,64,512]{2,1,0:T(8,128)S(1)} custom-call(f32[8]{0:T(128)S(1)} %copy-done, f32[48,64,2048]{2,1,0:T(8,128)} %volume.11, f32[1,64,2048]{2,1,0:T(8,128)S(1)} %collective-permute-done.refs_0_, f32[1,64,2048]{2,1,0:T(8,128)S(1)} %collective-permute-done.1.refs_1_, f32[48,1,2048]{2,1,0:T(1,128)S(1)} %collective-permute-done.2.refs_2_, ...), custom_call_target="tpu_custom_call" | custom-call | tf_op jit(solution)/shard_map/pallas_call | solution.py:333
  50.9 0.3 collective-permute-start.4
  51.2 9.3 %shard_map.32.refs_3_ = f32[3,64,512]{2,1,0:T(8,128)S(1)} custom-call(f32[8]{0:T(128)S(1)} %copy-done, f32[48,64,2048]{2,1,0:T(8,128)} %volume.11, f32[1,64,2048]{2,1,0:T(8,128)S(1)} %collective-permute-done.refs_0_, f32[1,64,2048]{2,1,0:T(8,128)S(1)} %collective-permute-done.1.refs_1_, f32[48,1,2048]{2,1,0:T(1,128)S(1)} %collective-permute-done.2.refs_2_, ...), custom_call_target="tpu_custom_call" | custom-call | tf_op jit(solution)/shard_map/pallas_call | solution.py:333
  60.5 0.0 collective-permute-done.5.refs_1_
  60.5 0.0 collective-permute-done.6.refs_2_
  60.5 13.0 %collective-permute-done.4.refs_0_ = f32[3,64,512]{2,1,0:T(8,128)S(1)} collective-permute-done((f32[3,64,512]{2,1,0:T(8,128)S(1)}, f32[3,64,512]{2,1,0:T(8,128)S(1)}, u32[]{:S(2)}, u32[]{:S(2)}) %collective-permute-start.4) | collective-permute-done | bytes 393248 | tf_op jit(solution)/shard_map/ppermute | solution.py:424
  73.5 1.8 %merge.1 = f32[4,64,512]{2,1,0:T(8,128)} custom-call(f32[8]{0:T(128)S(1)} %copy-done, f32[3,64,512]{2,1,0:T(8,128)S(1)} %collective-permute-done.4.refs_0_, f32[3,64,512]{2,1,0:T(8,128)S(1)} %collective-permute-done.5.refs_1_, f32[3,64,512]{2,1,0:T(8,128)S(1)} %collective-permute-done.6.refs_2_, f32[3,64,512]{2,1,0:T(8,128)S(1)} %shard_map.32.refs_3_), custom_call_target="tpu_custom_call" | custom-call | tf_op jit(solution)/shard_map/merge/pallas_call | solution.py:381
Async XLA Ops:
  0.0 11.8 %copy-start = (f32[8]{0:T(128)S(1)}, f32[8]{0:T(128)}, u32[]{:S(2)}) copy-start(f32[8]{0:T(128)} %transfer.11) | copy-start | bytes 100
  2.7 16.8 %collective-permute-start = (f32[1,64,2048]{2,1,0:T(8,128)}, f32[1,64,2048]{2,1,0:T(8,128)S(1)}, u32[]{:S(2)}, u32[]{:S(2)}) collective-permute-start(f32[1,64,2048]{2,1,0:T(8,128)} %get-tuple-element.9), channel_id=1, source_target_pairs={{0,8},{8,16},{16,24},{1,9},{9,17},{17,25},{2,10},{10,18},{18,26},{... | collective-permute-start | bytes 1572872 | tf_op jit(solution)/shard_map/ppermute | solution.py:56
  7.7 15.5 %collective-permute-start.1 = (f32[1,64,2048]{2,1,0:T(8,128)}, f32[1,64,2048]{2,1,0:T(8,128)S(1)}, u32[]{:S(2)}, u32[]{:S(2)}) collective-permute-start(f32[1,64,2048]{2,1,0:T(8,128)} %get-tuple-element.10), channel_id=1, source_target_pairs={{8,0},{16,8},{24,16},{9,1},{17,9},{25,17},{10,2},{18,10},{26,18},{... | collective-permute-start | bytes 1572872 | tf_op jit(solution)/shard_map/ppermute | solution.py:56
  9.0 10.5 %collective-permute-start.2 = (f32[48,1,2048]{2,1,0:T(1,128)}, f32[48,1,2048]{2,1,0:T(1,128)S(1)}, u32[]{:S(2)}, u32[]{:S(2)}) collective-permute-start(f32[48,1,2048]{2,1,0:T(1,128)} %get-tuple-element.11), channel_id=1, source_target_pairs={{0,1},{1,2},{2,3},{3,4},{4,5},{5,6},{6,7},{8,9},{9,10},{10,11},{11... | collective-permute-start | bytes 1179656 | tf_op jit(solution)/shard_map/ppermute | solution.py:56
  10.5 9.0 %collective-permute-start.3 = (f32[48,1,2048]{2,1,0:T(1,128)}, f32[48,1,2048]{2,1,0:T(1,128)S(1)}, u32[]{:S(2)}, u32[]{:S(2)}) collective-permute-start(f32[48,1,2048]{2,1,0:T(1,128)} %get-tuple-element.12), channel_id=1, source_target_pairs={{1,0},{2,1},{3,2},{4,3},{5,4},{6,5},{7,6},{9,8},{10,9},{11,10},{12... | collective-permute-start | bytes 1179656 | tf_op jit(solution)/shard_map/ppermute | solution.py:56
  32.8 27.7 %collective-permute-start.5 = (f32[3,64,512]{2,1,0:T(8,128)S(1)}, f32[3,64,512]{2,1,0:T(8,128)S(1)}, u32[]{:S(2)}, u32[]{:S(2)}) collective-permute-start(f32[3,64,512]{2,1,0:T(8,128)S(1)} %shard_map.30), channel_id=1, source_target_pairs={{0,8},{8,16},{16,24},{24,0},{1,9},{9,17},{17,25},{25,1},{2,10},{10... | collective-permute-start | bytes 1179656 | tf_op jit(solution)/shard_map/ppermute | solution.py:424
  43.9 16.6 %collective-permute-start.6 = (f32[3,64,512]{2,1,0:T(8,128)S(1)}, f32[3,64,512]{2,1,0:T(8,128)S(1)}, u32[]{:S(2)}, u32[]{:S(2)}) collective-permute-start(f32[3,64,512]{2,1,0:T(8,128)S(1)} %shard_map.31), channel_id=1, source_target_pairs={{0,24},{8,0},{16,8},{24,16},{1,25},{9,1},{17,9},{25,17},{2,26},{10... | collective-permute-start | bytes 1179656 | tf_op jit(solution)/shard_map/ppermute | solution.py:424
  50.9 22.6 %collective-permute-start.4 = (f32[3,64,512]{2,1,0:T(8,128)S(1)}, f32[3,64,512]{2,1,0:T(8,128)S(1)}, u32[]{:S(2)}, u32[]{:S(2)}) collective-permute-start(f32[3,64,512]{2,1,0:T(8,128)S(1)} %shard_map.29), channel_id=1, source_target_pairs={{0,16},{8,24},{16,0},{24,8},{1,17},{9,25},{17,1},{25,9},{2,18},{10... | collective-permute-start | bytes 1179656 | tf_op jit(solution)/shard_map/ppermute | solution.py:424

commit v4 on v3

--- a/solution.py
+++ b/solution.py
@@ -110,11 +110,11 @@
 
 
 class Bricks:
-    def __init__(self, volume, cells, sems, shift, chunks, pieces):
+    def __init__(self, volume, cells, sems, flip, chunks, pieces):
         self.volume, self.cells, self.sems, self.pieces = volume, cells, sems, pieces
         self.chunks = chunks
         self.total = volume.shape[2] // LANES
-        block = lax.rem(lax.axis_index("depth") + shift, lax.axis_size("depth"))
+        block = lax.bitwise_xor(lax.axis_index("depth"), jnp.int32(flip))
         self.base = block * chunks
         self.has_left = self.base > 0
         self.has_right = self.base + chunks < self.total
@@ -210,13 +210,13 @@
     return lax.fori_loop(0, trips, trip, carry)[0]
 
 
-def full_kernel(shift, tiles, pieces, total_slices, transfer, volume, *refs):
+def full_kernel(flip, tiles, pieces, total_slices, transfer, volume, *refs):
     *edges, out, cells, sems, edge_sems = refs
     slices, rows, _ = volume.shape
     chunks = out.shape[2] // LANES
     trips = len(pieces)
     groups = rows // SUBLANES // tiles
-    bricks = Bricks(volume, cells, sems, shift, chunks, pieces)
+    bricks = Bricks(volume, cells, sems, flip, chunks, pieces)
     for copy in edge_copies(bricks, edges, edge_sems, 1):
         copy.start()
     bricks.start_all()
@@ -250,11 +250,11 @@
     lax.fori_loop(0, chunks * groups, group, 0)
 
 
-def inner_kernel(shift, pieces, total_slices, transfer, volume, out, cells, sems):
+def inner_kernel(flip, pieces, total_slices, transfer, volume, out, cells, sems):
     slices, rows, _ = volume.shape
     chunks = out.shape[2] // LANES
     trips = len(pieces)
-    bricks = Bricks(volume, cells, sems, shift, chunks, pieces)
+    bricks = Bricks(volume, cells, sems, flip, chunks, pieces)
     bricks.start_all()
     coef = coefficients(transfer, total_slices)
     ends = tile_constants()
@@ -278,11 +278,11 @@
     lax.fori_loop(0, chunks, group, 0)
 
 
-def rest_kernel(shift, pieces, total_slices, transfer, volume, *refs):
+def rest_kernel(flip, pieces, total_slices, transfer, volume, *refs):
     *edges, inner, out, cells, sems, edge_sems = refs
     slices, rows, _ = volume.shape
     chunks = out.shape[2] // LANES
-    bricks = Bricks(volume, cells, sems, shift, chunks, pieces)
+    bricks = Bricks(volume, cells, sems, flip, chunks, pieces)
     for copy in edge_copies(bricks, edges, edge_sems, 1):
         copy.start()
     bricks.start_all()
@@ -340,12 +340,12 @@
     )(transfer, volume, *extra)
 
 
-def merge_kernel(shifts, transfer, *refs):
+def merge_kernel(flips, transfer, *refs):
     *parts, out = refs
     count = len(parts)
     mine = lax.axis_index("depth")
     rows, width = out.shape[1:]
-    sources = [lax.rem(mine - shift + count, count) for shift in shifts]
+    sources = [lax.bitwise_xor(mine, jnp.int32(flip)) for flip in flips]
     nearer = [
         [jnp.where(sources[j] < sources[i], 1.0, 0.0) for j in range(count)] for i in range(count)
     ]
@@ -376,16 +376,52 @@
     lax.fori_loop(0, rows // SUBLANES, band, 0)
 
 
-def merge(parts, shifts, transfer):
+def merge(parts, flips, transfer):
     _, rows, width = parts[0].shape
     return pl.pallas_call(
-        functools.partial(merge_kernel, shifts),
+        functools.partial(merge_kernel, flips),
         in_specs=[SMEM] + [VMEM] * len(parts),
         out_specs=VMEM,
         out_shape=jax.ShapeDtypeStruct((4, rows, width), jnp.float32),
         compiler_params=pltpu.CompilerParams(vmem_limit_bytes=16 << 20),
         name="merge",
     )(transfer, *parts)
+
+
+def fold_kernel(own, passed, out):
+    rows, width = out.shape[1:]
+    from_front = lax.axis_index("depth") < lax.axis_size("depth") // 2
+
+    def band(r, carry):
+        here = pl.ds(pl.multiple_of(r * SUBLANES, SUBLANES), SUBLANES)
+        for x in range(width // LANES):
+            at = pl.ds(x * LANES, LANES)
+            log_own, log_passed = own[2, here, at], passed[2, here, at]
+            passing = jnp.exp2(jnp.where(from_front, log_passed, log_own))
+            for channel in range(2):
+                a, b = own[channel, here, at], passed[channel, here, at]
+                front, back = jnp.where(from_front, b, a), jnp.where(from_front, a, b)
+                out[channel, here, at] = front + passing * back
+            out[2, here, at] = log_own + log_passed
+        return carry
+
+    lax.fori_loop(0, rows // SUBLANES, band, 0)
+
+
+def fold(own, passed):
+    return pl.pallas_call(
+        fold_kernel,
+        in_specs=[VMEM, VMEM],
+        out_specs=VMEM,
+        out_shape=jax.ShapeDtypeStruct(own.shape, jnp.float32),
+        compiler_params=pltpu.CompilerParams(vmem_limit_bytes=16 << 20),
+        name="fold",
+    )(own, passed)
+
+
+def exchange(part, groups, flip, members=None):
+    pairs = [(i, i ^ flip) for i in range(groups) if members is None or i in members]
+    return lax.ppermute(part, "depth", pairs)
 
 
 def on_device(volume, transfer):
@@ -403,31 +439,34 @@
     half = slices // 2
     halves = [(0, half + 1, 0, rows), (half + 1, slices - half - 1, 0, rows)]
     ring = [
-        (0, slices, 0, 2 * SUBLANES),
-        (0, slices, rows - 2 * SUBLANES, 2 * SUBLANES),
-        (0, 2, 2 * SUBLANES, rows - 4 * SUBLANES),
-        (slices - 2, 2, 2 * SUBLANES, rows - 4 * SUBLANES),
+        (0, slices, 0, SUBLANES),
+        (2, slices - 4, SUBLANES, 1),
+        (2, slices - 4, rows - SUBLANES - 1, 1),
+        (0, slices, rows - SUBLANES, SUBLANES),
+        (0, 2, SUBLANES, rows - 2 * SUBLANES),
+        (slices - 2, 2, SUBLANES, rows - 2 * SUBLANES),
     ]
-    shifts = order_of_shifts(groups)
+    flips = list(range(groups - 1, -1, -1))
+    hop = groups == 4
     parts = []
-    for stage, shift in enumerate(shifts):
+    for stage, flip in enumerate(flips):
         if stage == 0:
-            kernel = functools.partial(inner_kernel, shift, halves, total_slices)
+            kernel = functools.partial(inner_kernel, flip, halves, total_slices)
             inner = render(kernel, halves, transfer, volume, (), width, False)
-            kernel = functools.partial(rest_kernel, shift, ring, total_slices)
+            kernel = functools.partial(rest_kernel, flip, ring, total_slices)
             part = render(kernel, ring, transfer, volume, edges + (inner,), width, True)
         else:
-            kernel = functools.partial(full_kernel, shift, 8, halves, total_slices)
+            kernel = functools.partial(full_kernel, flip, 8, halves, total_slices)
             part = render(kernel, halves, transfer, volume, edges, width, True)
-        if shift:
-            pairs = [(i, (i + shift) % groups) for i in range(groups)]
-            part = lax.ppermute(part, "depth", pairs)
+        if hop and stage == 0:
+            passed = lax.ppermute(part, "depth", [(0, 1), (3, 2)])
+            part = exchange(part, groups, flip, (1, 2))
+        elif flip:
+            if hop and stage == 1:
+                part = fold(part, passed)
+            part = exchange(part, groups, flip)
         parts.append(part)
-    return merge(parts, shifts, transfer)
-
-
-def order_of_shifts(groups):
-    return sorted(range(1, groups), key=lambda s: -min(s, groups - s)) + [0]
+    return merge(parts, flips, transfer)
 
 
 def solution(mesh):

time: 75.4 us -> 75.9 us (level)
  starting transfers between devices: 13.3 us -> 16.1 us
  waiting for transfers between devices: 16.7 us -> 14.2 us
    ppermute x3 -> x4, starting transfers between devices: 4.24 us -> 7.07 us  [the longest x3 3.59 us: exchange(): return lax.ppermute(part, 'depth', pairs)]
    ppermute x3 -> x4, waiting for transfers between devices: 13 us -> 10.5 us  [the longest x3 10.5 us: exchange(): return lax.ppermute(part, 'depth', pairs)]
    pallas_call x1 -> x2, Pallas kernels: 1.75 us -> 1.86 us  [the longest x1 1.75 us: merge(): pl.pallas_call(functools.partial(merge_kernel, flips), in_specs=[SMEM] +...]
  transfers between devices with their start and end apart: 7 -> 8, of which waited for: 2 -> 2; matrix products, arithmetic and copies ran while one was open for 0% -> 0% of each run, Pallas kernels for 41% -> 48%
where the time goes in v4:
time: 75.9 us; the launch traced here: 75.7 us
  Pallas kernels  45.2 us (60%)
  starting transfers between devices  16.1 us (21%)
  waiting for transfers between devices  14.2 us (19%)
    pallas_call x5, Pallas kernels, render(): pl.pallas_call(kernel, in_specs=[SMEM, ANY] + [ANY] * min(4, len(extra))...  40.6 us
    ppermute x3, waiting for transfers between devices, exchange(): return lax.ppermute(part, 'depth', pairs)  10.5 us
    ppermute x4, starting transfers between devices, pass_on(): return lax.ppermute(value, axis, pairs)  9.06 us
    ppermute x4, waiting for transfers between devices, pass_on(): return lax.ppermute(value, axis, pairs)  3.7 us
    ppermute x3, starting transfers between devices, exchange(): return lax.ppermute(part, 'depth', pairs)  3.59 us
    ppermute x1, starting transfers between devices, on_device(): passed = lax.ppermute(part, 'depth', [(0, 1), (3, 2)])  3.48 us
    pallas_call x1, Pallas kernels, cut(): pl.pallas_call(cut_kernel, in_specs=[ANY], out_specs=[VMEM] * 4, out_shap...  2.71 us
    pallas_call x1, Pallas kernels, merge(): pl.pallas_call(functools.partial(merge_kernel, flips), in_specs=[SMEM] +...  1.75 us
  transfers between devices with their start and end apart: 8, of which 2 were waited for; matrix products, arithmetic and copies ran while one was open for 0% of the time, Pallas kernels for 48%

profile of v4, /device:TPU:0, one launch (start us, length us, event | category | flops | bytes accessed | tf_op | source)
XLA Modules:
  0.0 75.7 jit_solution(1554684170988509967)
XLA Ops:
  0.0 0.0 copy-start
  0.0 2.7 %cut.1 = (f32[1,64,2048]{2,1,0:T(8,128)}, f32[1,64,2048]{2,1,0:T(8,128)}, f32[48,1,2048]{2,1,0:T(1,128)}, f32[48,1,2048]{2,1,0:T(1,128)}) custom-call(f32[48,64,2048]{2,1,0:T(8,128)} %volume.11), custom_call_target="tpu_custom_call" | custom-call | tf_op jit(solution)/shard_map/cut/pallas_call | solution.py:43
  2.7 5.0 %collective-permute-start = (f32[1,64,2048]{2,1,0:T(8,128)}, f32[1,64,2048]{2,1,0:T(8,128)S(1)}, u32[]{:S(2)}, u32[]{:S(2)}) collective-permute-start(f32[1,64,2048]{2,1,0:T(8,128)} %get-tuple-element.9), channel_id=1, source_target_pairs={{0,8},{8,16},{16,24},{1,9},{9,17},{17,25},{2,10},{10,18},{18,26},{... | collective-permute-start | bytes 1572872 | tf_op jit(solution)/shard_map/ppermute | solution.py:56
  7.7 1.3 %collective-permute-start.1 = (f32[1,64,2048]{2,1,0:T(8,128)}, f32[1,64,2048]{2,1,0:T(8,128)S(1)}, u32[]{:S(2)}, u32[]{:S(2)}) collective-permute-start(f32[1,64,2048]{2,1,0:T(8,128)} %get-tuple-element.10), channel_id=1, source_target_pairs={{8,0},{16,8},{24,16},{9,1},{17,9},{25,17},{10,2},{18,10},{26,18},{... | collective-permute-start | bytes 1572872 | tf_op jit(solution)/shard_map/ppermute | solution.py:56
  9.0 1.5 %collective-permute-start.2 = (f32[48,1,2048]{2,1,0:T(1,128)}, f32[48,1,2048]{2,1,0:T(1,128)S(1)}, u32[]{:S(2)}, u32[]{:S(2)}) collective-permute-start(f32[48,1,2048]{2,1,0:T(1,128)} %get-tuple-element.11), channel_id=1, source_target_pairs={{0,1},{1,2},{2,3},{3,4},{4,5},{5,6},{6,7},{8,9},{9,10},{10,11},{11... | collective-permute-start | bytes 1179656 | tf_op jit(solution)/shard_map/ppermute | solution.py:56
  10.5 1.3 %collective-permute-start.3 = (f32[48,1,2048]{2,1,0:T(1,128)}, f32[48,1,2048]{2,1,0:T(1,128)S(1)}, u32[]{:S(2)}, u32[]{:S(2)}) collective-permute-start(f32[48,1,2048]{2,1,0:T(1,128)} %get-tuple-element.12), channel_id=1, source_target_pairs={{1,0},{2,1},{3,2},{4,3},{5,4},{6,5},{7,6},{9,8},{10,9},{11,10},{12... | collective-permute-start | bytes 1179656 | tf_op jit(solution)/shard_map/ppermute | solution.py:56
  11.8 0.0 copy-done
  11.8 7.7 %shard_map.28.refs_4_ = f32[3,64,512]{2,1,0:T(8,128)S(1)} custom-call(f32[8]{0:T(128)S(1)} %copy-done, f32[48,64,2048]{2,1,0:T(8,128)} %volume.11), custom_call_target="tpu_custom_call" | custom-call | tf_op jit(solution)/shard_map/pallas_call | solution.py:333
  19.5 0.0 collective-permute-done.2.refs_2_
  19.5 0.0 collective-permute-done.3.refs_3_
  19.5 0.0 collective-permute-done.refs_0_
  19.5 3.7 %collective-permute-done.1.refs_1_ = f32[1,64,2048]{2,1,0:T(8,128)S(1)} collective-permute-done((f32[1,64,2048]{2,1,0:T(8,128)}, f32[1,64,2048]{2,1,0:T(8,128)S(1)}, u32[]{:S(2)}, u32[]{:S(2)}) %collective-permute-start.1) | collective-permute-done | bytes 524320 | tf_op jit(solution)/shard_map/ppermute | solution.py:56
  23.2 4.6 %shard_map.29 = f32[3,64,512]{2,1,0:T(8,128)S(1)} custom-call(f32[8]{0:T(128)S(1)} %copy-done, f32[48,64,2048]{2,1,0:T(8,128)} %volume.11, f32[1,64,2048]{2,1,0:T(8,128)S(1)} %collective-permute-done.refs_0_, f32[1,64,2048]{2,1,0:T(8,128)S(1)} %collective-permute-done.1.refs_1_, f32[48,1,2048]{2,1,0:T(1,128)S(1)} %collective-permute-done.2.refs_2_, ...), custom_call_target="tpu_custom_call" | custom-call | tf_op jit(solution)/shard_map/pallas_call | solution.py:333
  27.8 3.5 %collective-permute-start.5 = (f32[3,64,512]{2,1,0:T(8,128)S(1)}, f32[3,64,512]{2,1,0:T(8,128)S(1)}, u32[]{:S(2)}, u32[]{:S(2)}) collective-permute-start(f32[3,64,512]{2,1,0:T(8,128)S(1)} %shard_map.29), channel_id=1, source_target_pairs={{0,8},{24,16},{1,9},{25,17},{2,10},{26,18},{3,11},{27,19},{4,12},{... | collective-permute-start | bytes 1179656 | tf_op jit(solution)/shard_map/ppermute | solution.py:462
  31.3 0.7 collective-permute-start.4
  32.0 9.5 %shard_map.31 = f32[3,64,512]{2,1,0:T(8,128)S(1)} custom-call(f32[8]{0:T(128)S(1)} %copy-done, f32[48,64,2048]{2,1,0:T(8,128)} %volume.11, f32[1,64,2048]{2,1,0:T(8,128)S(1)} %collective-permute-done.refs_0_, f32[1,64,2048]{2,1,0:T(8,128)S(1)} %collective-permute-done.1.refs_1_, f32[48,1,2048]{2,1,0:T(1,128)S(1)} %collective-permute-done.2.refs_2_, ...), custom_call_target="tpu_custom_call" | custom-call | tf_op jit(solution)/shard_map/pallas_call | solution.py:333
  41.5 2.0 %collective-permute-start.7 = (f32[3,64,512]{2,1,0:T(8,128)S(1)}, f32[3,64,512]{2,1,0:T(8,128)S(1)}, u32[]{:S(2)}, u32[]{:S(2)}) collective-permute-start(f32[3,64,512]{2,1,0:T(8,128)S(1)} %shard_map.31), channel_id=1, source_target_pairs={{0,8},{8,0},{16,24},{24,16},{1,9},{9,1},{17,25},{25,17},{2,10},{10... | collective-permute-start | bytes 1179656 | tf_op jit(solution)/shard_map/ppermute | solution.py:424
  43.5 9.5 %shard_map.30.own = f32[3,64,512]{2,1,0:T(8,128)S(1)} custom-call(f32[8]{0:T(128)S(1)} %copy-done, f32[48,64,2048]{2,1,0:T(8,128)} %volume.11, f32[1,64,2048]{2,1,0:T(8,128)S(1)} %collective-permute-done.refs_0_, f32[1,64,2048]{2,1,0:T(8,128)S(1)} %collective-permute-done.1.refs_1_, f32[48,1,2048]{2,1,0:T(1,128)S(1)} %collective-permute-done.2.refs_2_, ...), custom_call_target="tpu_custom_call" | custom-call | tf_op jit(solution)/shard_map/pallas_call | solution.py:333
  53.0 0.0 collective-permute-done.5.passed
  53.0 0.1 fold.1
  53.2 0.9 %collective-permute-start.6 = (f32[3,64,512]{2,1,0:T(8,128)S(1)}, f32[3,64,512]{2,1,0:T(8,128)S(1)}, u32[]{:S(2)}, u32[]{:S(2)}) collective-permute-start(f32[3,64,512]{2,1,0:T(8,128)S(1)} %fold.1), channel_id=1, source_target_pairs={{0,16},{8,24},{16,0},{24,8},{1,17},{9,25},{17,1},{25,9},{2,18},{10... | collective-permute-start | bytes 1179656 | tf_op jit(solution)/shard_map/ppermute | solution.py:424
  54.1 9.3 %shard_map.32.refs_3_ = f32[3,64,512]{2,1,0:T(8,128)S(1)} custom-call(f32[8]{0:T(128)S(1)} %copy-done, f32[48,64,2048]{2,1,0:T(8,128)} %volume.11, f32[1,64,2048]{2,1,0:T(8,128)S(1)} %collective-permute-done.refs_0_, f32[1,64,2048]{2,1,0:T(8,128)S(1)} %collective-permute-done.1.refs_1_, f32[48,1,2048]{2,1,0:T(1,128)S(1)} %collective-permute-done.2.refs_2_, ...), custom_call_target="tpu_custom_call" | custom-call | tf_op jit(solution)/shard_map/pallas_call | solution.py:333
  63.4 0.0 collective-permute-done.7.refs_2_
  63.4 0.0 collective-permute-done.4.refs_0_
  63.4 10.5 %collective-permute-done.6.refs_1_ = f32[3,64,512]{2,1,0:T(8,128)S(1)} collective-permute-done((f32[3,64,512]{2,1,0:T(8,128)S(1)}, f32[3,64,512]{2,1,0:T(8,128)S(1)}, u32[]{:S(2)}, u32[]{:S(2)}) %collective-permute-start.6) | collective-permute-done | bytes 393248 | tf_op jit(solution)/shard_map/ppermute | solution.py:424
  73.9 1.7 %merge.1 = f32[4,64,512]{2,1,0:T(8,128)} custom-call(f32[8]{0:T(128)S(1)} %copy-done, f32[3,64,512]{2,1,0:T(8,128)S(1)} %collective-permute-done.4.refs_0_, f32[3,64,512]{2,1,0:T(8,128)S(1)} %collective-permute-done.6.refs_1_, f32[3,64,512]{2,1,0:T(8,128)S(1)} %collective-permute-done.7.refs_2_, f32[3,64,512]{2,1,0:T(8,128)S(1)} %shard_map.32.refs_3_), custom_call_target="tpu_custom_call" | custom-call | tf_op jit(solution)/shard_map/merge/pallas_call | solution.py:381
Async XLA Ops:
  0.0 11.8 %copy-start = (f32[8]{0:T(128)S(1)}, f32[8]{0:T(128)}, u32[]{:S(2)}) copy-start(f32[8]{0:T(128)} %transfer.11) | copy-start | bytes 100
  2.7 16.8 %collective-permute-start = (f32[1,64,2048]{2,1,0:T(8,128)}, f32[1,64,2048]{2,1,0:T(8,128)S(1)}, u32[]{:S(2)}, u32[]{:S(2)}) collective-permute-start(f32[1,64,2048]{2,1,0:T(8,128)} %get-tuple-element.9), channel_id=1, source_target_pairs={{0,8},{8,16},{16,24},{1,9},{9,17},{17,25},{2,10},{10,18},{18,26},{... | collective-permute-start | bytes 1572872 | tf_op jit(solution)/shard_map/ppermute | solution.py:56
  7.7 15.5 %collective-permute-start.1 = (f32[1,64,2048]{2,1,0:T(8,128)}, f32[1,64,2048]{2,1,0:T(8,128)S(1)}, u32[]{:S(2)}, u32[]{:S(2)}) collective-permute-start(f32[1,64,2048]{2,1,0:T(8,128)} %get-tuple-element.10), channel_id=1, source_target_pairs={{8,0},{16,8},{24,16},{9,1},{17,9},{25,17},{10,2},{18,10},{26,18},{... | collective-permute-start | bytes 1572872 | tf_op jit(solution)/shard_map/ppermute | solution.py:56
  9.0 10.5 %collective-permute-start.2 = (f32[48,1,2048]{2,1,0:T(1,128)}, f32[48,1,2048]{2,1,0:T(1,128)S(1)}, u32[]{:S(2)}, u32[]{:S(2)}) collective-permute-start(f32[48,1,2048]{2,1,0:T(1,128)} %get-tuple-element.11), channel_id=1, source_target_pairs={{0,1},{1,2},{2,3},{3,4},{4,5},{5,6},{6,7},{8,9},{9,10},{10,11},{11... | collective-permute-start | bytes 1179656 | tf_op jit(solution)/shard_map/ppermute | solution.py:56
  10.5 9.0 %collective-permute-start.3 = (f32[48,1,2048]{2,1,0:T(1,128)}, f32[48,1,2048]{2,1,0:T(1,128)S(1)}, u32[]{:S(2)}, u32[]{:S(2)}) collective-permute-start(f32[48,1,2048]{2,1,0:T(1,128)} %get-tuple-element.12), channel_id=1, source_target_pairs={{1,0},{2,1},{3,2},{4,3},{5,4},{6,5},{7,6},{9,8},{10,9},{11,10},{12... | collective-permute-start | bytes 1179656 | tf_op jit(solution)/shard_map/ppermute | solution.py:56
  27.8 25.2 %collective-permute-start.5 = (f32[3,64,512]{2,1,0:T(8,128)S(1)}, f32[3,64,512]{2,1,0:T(8,128)S(1)}, u32[]{:S(2)}, u32[]{:S(2)}) collective-permute-start(f32[3,64,512]{2,1,0:T(8,128)S(1)} %shard_map.29), channel_id=1, source_target_pairs={{0,8},{24,16},{1,9},{25,17},{2,10},{26,18},{3,11},{27,19},{4,12},{... | collective-permute-start | bytes 1179656 | tf_op jit(solution)/shard_map/ppermute | solution.py:462
  31.3 32.1 %collective-permute-start.4 = (f32[3,64,512]{2,1,0:T(8,128)S(1)}, f32[3,64,512]{2,1,0:T(8,128)S(1)}, u32[]{:S(2)}, u32[]{:S(2)}) collective-permute-start(f32[3,64,512]{2,1,0:T(8,128)S(1)} %shard_map.29), channel_id=1, source_target_pairs={{8,16},{16,8},{9,17},{17,9},{10,18},{18,10},{11,19},{19,11},{12,20... | collective-permute-start | bytes 1179656 | tf_op jit(solution)/shard_map/ppermute | solution.py:424
  41.5 21.9 %collective-permute-start.7 = (f32[3,64,512]{2,1,0:T(8,128)S(1)}, f32[3,64,512]{2,1,0:T(8,128)S(1)}, u32[]{:S(2)}, u32[]{:S(2)}) collective-permute-start(f32[3,64,512]{2,1,0:T(8,128)S(1)} %shard_map.31), channel_id=1, source_target_pairs={{0,8},{8,0},{16,24},{24,16},{1,9},{9,1},{17,25},{25,17},{2,10},{10... | collective-permute-start | bytes 1179656 | tf_op jit(solution)/shard_map/ppermute | solution.py:424
  53.2 20.8 %collective-permute-start.6 = (f32[3,64,512]{2,1,0:T(8,128)S(1)}, f32[3,64,512]{2,1,0:T(8,128)S(1)}, u32[]{:S(2)}, u32[]{:S(2)}) collective-permute-start(f32[3,64,512]{2,1,0:T(8,128)S(1)} %fold.1), channel_id=1, source_target_pairs={{0,16},{8,24},{16,0},{24,8},{1,17},{9,25},{17,1},{25,9},{2,18},{10... | collective-permute-start | bytes 1179656 | tf_op jit(solution)/shard_map/ppermute | solution.py:424

commit v5 on v3

--- a/solution.py
+++ b/solution.py
@@ -172,19 +172,37 @@
             self.copy(c + 1, k).wait()
 
 
-def edge_copies(bricks, edges, sems, c):
-    before, after, above_row, below_row = edges
-    slices, rows, _ = bricks.volume.shape
-    cells, at = bricks.cells, bricks.lanes(c)
-    inner = pl.ds(SUBLANES, rows)
-    middle = pl.ds(1, slices)
-    pairs = [
-        (before.at[0, :, at], cells.at[c, 0, inner, :]),
-        (after.at[0, :, at], cells.at[c, slices + 1, inner, :]),
-        (above_row.at[:, :, at], cells.at[c, middle, pl.ds(SUBLANES - 1, 1), :]),
-        (below_row.at[:, :, at], cells.at[c, middle, pl.ds(SUBLANES + rows, 1), :]),
-    ]
-    return [pltpu.make_async_copy(*pair, sems.at[c, i]) for i, pair in enumerate(pairs)]
+class Edges:
+    def __init__(self, bricks, sems, slabs, strips, spans):
+        self.bricks, self.sems, self.slabs, self.strips, self.spans = bricks, sems, slabs, strips, spans
+
+    def copies(self, c):
+        slices, rows, _ = self.bricks.volume.shape
+        cells, at = self.bricks.cells, self.bricks.lanes(c)
+        pairs = []
+        for slab, z in zip(self.slabs, (0, slices + 1)):
+            pairs.append((slab.at[0, :, at], cells.at[c, z, pl.ds(SUBLANES, rows), :]))
+        for strip, row in zip(self.strips, (SUBLANES - 1, SUBLANES + rows)):
+            for z, size in self.spans:
+                pairs.append(
+                    (strip.at[pl.ds(z, size), :, at], cells.at[c, pl.ds(z + 1, size), pl.ds(row, 1), :])
+                )
+        return [pltpu.make_async_copy(*pair, self.sems.at[c, i]) for i, pair in enumerate(pairs)]
+
+    def start(self, c):
+        for copy in self.copies(c):
+            copy.start()
+
+    def wait(self, c):
+        for copy in self.copies(c):
+            copy.wait()
+
+
+def start_everything(bricks, edges):
+    edges.start(1)
+    bricks.start_all()
+    for c in range(2, bricks.chunks + 1):
+        edges.start(c)
 
 
 def march(cells, c, rows, begin, step, trips, coef, ends, arrive):
@@ -211,18 +229,14 @@
 
 
 def full_kernel(shift, tiles, pieces, total_slices, transfer, volume, *refs):
-    *edges, out, cells, sems, edge_sems = refs
+    before, after, above_row, below_row, out, cells, sems, edge_sems = refs
     slices, rows, _ = volume.shape
     chunks = out.shape[2] // LANES
     trips = len(pieces)
     groups = rows // SUBLANES // tiles
     bricks = Bricks(volume, cells, sems, shift, chunks, pieces)
-    for copy in edge_copies(bricks, edges, edge_sems, 1):
-        copy.start()
-    bricks.start_all()
-    for c in range(2, chunks + 1):
-        for copy in edge_copies(bricks, edges, edge_sems, c):
-            copy.start()
+    edges = Edges(bricks, edge_sems, (before, after), (above_row, below_row), [(0, slices)])
+    start_everything(bricks, edges)
     coef = coefficients(transfer, total_slices)
     ends = tile_constants()
 
@@ -233,8 +247,7 @@
 
         @pl.when(fresh)
         def _():
-            for copy in edge_copies(bricks, edges, edge_sems, c):
-                copy.wait()
+            edges.wait(c)
             bricks.land(c, 0)
 
         def arrive(k):
@@ -278,32 +291,49 @@
     lax.fori_loop(0, chunks, group, 0)
 
 
-def rest_kernel(shift, pieces, total_slices, transfer, volume, *refs):
-    *edges, inner, out, cells, sems, edge_sems = refs
+def outer_kernel(shift, pieces, total_slices, transfer, volume, *refs):
+    above_row, below_row, out, cells, sems, edge_sems = refs
     slices, rows, _ = volume.shape
     chunks = out.shape[2] // LANES
     bricks = Bricks(volume, cells, sems, shift, chunks, pieces)
-    for copy in edge_copies(bricks, edges, edge_sems, 1):
-        copy.start()
-    bricks.start_all()
-    for c in range(2, chunks + 1):
-        for copy in edge_copies(bricks, edges, edge_sems, c):
-            copy.start()
+    edges = Edges(bricks, edge_sems, (), (above_row, below_row), [(0, slices)])
+    start_everything(bricks, edges)
     coef = coefficients(transfer, total_slices)
     ends = tile_constants()
 
     def group(index, carry):
         c = index + 1
-        for copy in edge_copies(bricks, edges, edge_sems, c):
-            copy.wait()
+        edges.wait(c)
         for k in range(len(pieces)):
             bricks.land(c, k)
-        outer = [SUBLANES, rows]
-        states = march(cells, c, outer, 0, slices, 1, coef, ends, lambda k: None)
-        for at_row, state in zip(outer, states):
-            put(out, c, at_row, state)
-        lanes = pl.ds(pl.multiple_of((c - 1) * LANES, LANES), LANES)
-        for t in range(1, rows // SUBLANES - 1):
+        at_rows = [SUBLANES, rows]
+        states = march(cells, c, at_rows, 1, slices - 2, 1, coef, ends, lambda k: None)
+        for place, state in enumerate(states):
+            put(out, c, SUBLANES * (place + 1), state)
+        return carry
+
+    lax.fori_loop(0, chunks, group, 0)
+
+
+def close_kernel(shift, pieces, total_slices, transfer, volume, *refs):
+    before, after, above_row, below_row, inner, outer, out, cells, sems, edge_sems = refs
+    slices, rows, _ = volume.shape
+    chunks = out.shape[2] // LANES
+    tiles = rows // SUBLANES
+    bricks = Bricks(volume, cells, sems, shift, chunks, pieces)
+    spans = [(0, 1), (slices - 1, 1)]
+    edges = Edges(bricks, edge_sems, (before, after), (above_row, below_row), spans)
+    start_everything(bricks, edges)
+    coef = coefficients(transfer, total_slices)
+    ends = tile_constants()
+
+    def group(index, carry):
+        c = index + 1
+        edges.wait(c)
+        for k in range(len(pieces)):
+            bricks.land(c, k)
+        lanes = pl.ds(pl.multiple_of(index * LANES, LANES), LANES)
+        for t in range(tiles):
             row = SUBLANES * (t + 1)
             here = pl.ds(row, SUBLANES)
             sides = []
@@ -311,7 +341,9 @@
                 below, x, above = [cells[c, z + i, here, :] for i in (-1, 0, 1)]
                 sides.append(cell(cells, c, z, row, x, below, above, fresh_state(), coef, ends))
             (log_a, pass_a, shade_a, tint_a), (log_b, _, shade_b, tint_b) = sides
-            shade, tint, log_t = [inner[i, pl.ds(row - SUBLANES, SUBLANES), lanes] for i in range(3)]
+            between, place = (inner, t) if 0 < t < tiles - 1 else (outer, min(t, 1))
+            held = pl.ds(SUBLANES * place, SUBLANES)
+            shade, tint, log_t = [between[i, held, lanes] for i in range(3)]
             passing = jnp.exp2(log_t)
             shade = shade_a + pass_a * (shade + passing * shade_b)
             tint = tint_a + pass_a * (tint + passing * tint_b)
@@ -321,7 +353,7 @@
     lax.fori_loop(0, chunks, group, 0)
 
 
-def render(kernel, pieces, transfer, volume, extra, width, halo):
+def render(kernel, pieces, transfer, volume, halo, done, width, out_rows=None):
     slices, rows, _ = volume.shape
     chunks = width // LANES
     scratch = [
@@ -329,19 +361,19 @@
         pltpu.SemaphoreType.DMA((chunks + 2, len(pieces))),
     ]
     if halo:
-        scratch.append(pltpu.SemaphoreType.DMA((chunks + 1, 4)))
+        scratch.append(pltpu.SemaphoreType.DMA((chunks + 1, 6)))
     return pl.pallas_call(
-        kernel,
-        in_specs=[SMEM, ANY] + [ANY] * min(4, len(extra)) + [VMEM] * (len(extra) - 4),
+        functools.partial(kernel, pieces, slices * lax.axis_size("depth")),
+        in_specs=[SMEM, ANY] + [ANY] * len(halo) + [VMEM] * len(done),
         out_specs=VMEM,
-        out_shape=jax.ShapeDtypeStruct((3, rows, width), jnp.float32),
+        out_shape=jax.ShapeDtypeStruct((3, out_rows or rows, width), jnp.float32),
         scratch_shapes=scratch,
         compiler_params=pltpu.CompilerParams(vmem_limit_bytes=32 << 20),
-    )(transfer, volume, *extra)
+    )(transfer, volume, *halo, *done)
 
 
 def merge_kernel(shifts, transfer, *refs):
-    *parts, out = refs
+    *parts, image, out, sems = refs
     count = len(parts)
     mine = lax.axis_index("depth")
     rows, width = out.shape[1:]
@@ -371,9 +403,16 @@
             for color in range(3):
                 out[color, here, at] = transfer[color] * full + transfer[3 + color] * mixed
             out[3, here, at] = opacity
+        copy(r).start()
         return carry
 
+    def copy(r):
+        here = pl.ds(pl.multiple_of(r * SUBLANES, SUBLANES), SUBLANES)
+        return pltpu.make_async_copy(out.at[:, here, :], image.at[:, here, :], sems.at[r])
+
     lax.fori_loop(0, rows // SUBLANES, band, 0)
+    for r in range(rows // SUBLANES):
+        copy(r).wait()
 
 
 def merge(parts, shifts, transfer):
@@ -381,8 +420,12 @@
     return pl.pallas_call(
         functools.partial(merge_kernel, shifts),
         in_specs=[SMEM] + [VMEM] * len(parts),
-        out_specs=VMEM,
+        out_specs=ANY,
         out_shape=jax.ShapeDtypeStruct((4, rows, width), jnp.float32),
+        scratch_shapes=[
+            pltpu.VMEM((4, rows, width), jnp.float32),
+            pltpu.SemaphoreType.DMA((rows // SUBLANES,)),
+        ],
         compiler_params=pltpu.CompilerParams(vmem_limit_bytes=16 << 20),
         name="merge",
     )(transfer, *parts)
@@ -391,34 +434,28 @@
 def on_device(volume, transfer):
     slices, rows, columns = volume.shape
     groups = lax.axis_size("depth")
-    total_slices = slices * groups
     width = columns // groups
     first, last, top, bottom = cut(volume)
-    edges = (
-        pass_on(last, "depth", True),
-        pass_on(first, "depth", False),
-        pass_on(bottom, "row", True),
-        pass_on(top, "row", False),
-    )
+    slabs = (pass_on(last, "depth", True), pass_on(first, "depth", False))
+    strips = (pass_on(bottom, "row", True), pass_on(top, "row", False))
     half = slices // 2
     halves = [(0, half + 1, 0, rows), (half + 1, slices - half - 1, 0, rows)]
-    ring = [
-        (0, slices, 0, 2 * SUBLANES),
-        (0, slices, rows - 2 * SUBLANES, 2 * SUBLANES),
-        (0, 2, 2 * SUBLANES, rows - 4 * SUBLANES),
-        (slices - 2, 2, 2 * SUBLANES, rows - 4 * SUBLANES),
-    ]
+    rim = [(0, slices, 0, 2 * SUBLANES), (0, slices, rows - 2 * SUBLANES, 2 * SUBLANES)]
+    caps = [(0, 2, 0, rows), (slices - 2, 2, 0, rows)]
     shifts = order_of_shifts(groups)
     parts = []
     for stage, shift in enumerate(shifts):
         if stage == 0:
-            kernel = functools.partial(inner_kernel, shift, halves, total_slices)
-            inner = render(kernel, halves, transfer, volume, (), width, False)
-            kernel = functools.partial(rest_kernel, shift, ring, total_slices)
-            part = render(kernel, ring, transfer, volume, edges + (inner,), width, True)
+            kernel = functools.partial(inner_kernel, shift)
+            inner = render(kernel, halves, transfer, volume, (), (), width)
+            kernel = functools.partial(outer_kernel, shift)
+            outer = render(kernel, rim, transfer, volume, strips, (), width, 2 * SUBLANES)
+            kernel = functools.partial(close_kernel, shift)
+            done = (inner, outer)
+            part = render(kernel, caps, transfer, volume, slabs + strips, done, width)
         else:
-            kernel = functools.partial(full_kernel, shift, 8, halves, total_slices)
-            part = render(kernel, halves, transfer, volume, edges, width, True)
+            kernel = functools.partial(full_kernel, shift, 8)
+            part = render(kernel, halves, transfer, volume, slabs + strips, (), width)
         if shift:
             pairs = [(i, (i + shift) % groups) for i in range(groups)]
             part = lax.ppermute(part, "depth", pairs)

time: 75.4 us -> 78.5 us (1.041)
  the two profiles are of different devices: /device:TPU:0 before, /device:TPU:3 now
where the time goes in v5:
time: 78.5 us; the launch traced here: 78.2 us
  Pallas kernels  47.5 us (61%)
  waiting for transfers between devices  15.7 us (20%)
  starting transfers between devices  14.9 us (19%)
    pallas_call x6, Pallas kernels, render(): pl.pallas_call(functools.partial(kernel, pieces, slices * lax.axis_size('...  43.1 us
    ppermute x3, waiting for transfers between devices, on_device(): part = lax.ppermute(part, 'depth', pairs)  14.5 us
    ppermute x4, starting transfers between devices, pass_on(): return lax.ppermute(value, axis, pairs)  10.4 us
    ppermute x3, starting transfers between devices, on_device(): part = lax.ppermute(part, 'depth', pairs)  4.53 us
    pallas_call x1, Pallas kernels, cut(): pl.pallas_call(cut_kernel, in_specs=[ANY], out_specs=[VMEM] * 4, out_shap...  2.72 us
    pallas_call x1, Pallas kernels, merge(): pl.pallas_call(functools.partial(merge_kernel, shifts), in_specs=[SMEM] +...  1.66 us
  transfers between devices with their start and end apart: 7, of which 2 were waited for; matrix products, arithmetic and copies ran while one was open for 0% of the time, Pallas kernels for 43%

profile of v5, /device:TPU:3, one launch (start us, length us, event | category | flops | bytes accessed | tf_op | source)
XLA Modules:
  0.0 78.2 jit_solution(8155039311393978452)
XLA Ops:
  0.0 0.0 copy-start
  0.0 2.7 %cut.1 = (f32[1,64,2048]{2,1,0:T(8,128)}, f32[1,64,2048]{2,1,0:T(8,128)}, f32[48,1,2048]{2,1,0:T(1,128)}, f32[48,1,2048]{2,1,0:T(1,128)}) custom-call(f32[48,64,2048]{2,1,0:T(8,128)} %volume.13), custom_call_target="tpu_custom_call" | custom-call | tf_op jit(solution)/shard_map/cut/pallas_call | solution.py:43
  2.7 3.2 %collective-permute-start = (f32[1,64,2048]{2,1,0:T(8,128)}, f32[1,64,2048]{2,1,0:T(8,128)S(1)}, u32[]{:S(2)}, u32[]{:S(2)}) collective-permute-start(f32[1,64,2048]{2,1,0:T(8,128)} %get-tuple-element.9), channel_id=1, source_target_pairs={{0,8},{8,16},{16,24},{1,9},{9,17},{17,25},{2,10},{10,18},{18,26},{... | collective-permute-start | bytes 1572872 | tf_op jit(solution)/shard_map/ppermute | solution.py:56
  6.0 1.3 %collective-permute-start.1 = (f32[1,64,2048]{2,1,0:T(8,128)}, f32[1,64,2048]{2,1,0:T(8,128)S(1)}, u32[]{:S(2)}, u32[]{:S(2)}) collective-permute-start(f32[1,64,2048]{2,1,0:T(8,128)} %get-tuple-element.10), channel_id=1, source_target_pairs={{8,0},{16,8},{24,16},{9,1},{17,9},{25,17},{10,2},{18,10},{26,18},{... | collective-permute-start | bytes 1572872 | tf_op jit(solution)/shard_map/ppermute | solution.py:56
  7.3 4.0 %collective-permute-start.2 = (f32[48,1,2048]{2,1,0:T(1,128)}, f32[48,1,2048]{2,1,0:T(1,128)S(1)}, u32[]{:S(2)}, u32[]{:S(2)}) collective-permute-start(f32[48,1,2048]{2,1,0:T(1,128)} %get-tuple-element.11), channel_id=1, source_target_pairs={{0,1},{1,2},{2,3},{3,4},{4,5},{5,6},{6,7},{8,9},{9,10},{10,11},{11... | collective-permute-start | bytes 1179656 | tf_op jit(solution)/shard_map/ppermute | solution.py:56
  11.2 1.9 %collective-permute-start.3 = (f32[48,1,2048]{2,1,0:T(1,128)}, f32[48,1,2048]{2,1,0:T(1,128)S(1)}, u32[]{:S(2)}, u32[]{:S(2)}) collective-permute-start(f32[48,1,2048]{2,1,0:T(1,128)} %get-tuple-element.12), channel_id=1, source_target_pairs={{1,0},{2,1},{3,2},{4,3},{5,4},{6,5},{7,6},{9,8},{10,9},{11,10},{12... | collective-permute-start | bytes 1179656 | tf_op jit(solution)/shard_map/ppermute | solution.py:56
  13.2 0.0 copy-done
  13.2 7.7 %shard_map.28.refs_4_ = f32[3,64,512]{2,1,0:T(8,128)S(1)} custom-call(f32[8]{0:T(128)S(1)} %copy-done, f32[48,64,2048]{2,1,0:T(8,128)} %volume.13), custom_call_target="tpu_custom_call" | custom-call | tf_op jit(solution)/shard_map/pallas_call | solution.py:365
  20.8 0.0 collective-permute-done.2.refs_0_.refs_2_
  20.9 1.2 %collective-permute-done.3.refs_1_.refs_3_ = f32[48,1,2048]{2,1,0:T(1,128)S(1)} collective-permute-done((f32[48,1,2048]{2,1,0:T(1,128)}, f32[48,1,2048]{2,1,0:T(1,128)S(1)}, u32[]{:S(2)}, u32[]{:S(2)}) %collective-permute-start.3) | collective-permute-done | bytes 393248 | tf_op jit(solution)/shard_map/ppermute | solution.py:56
  22.0 4.3 %shard_map.29.refs_5_ = f32[3,16,512]{2,1,0:T(8,128)S(1)} custom-call(f32[8]{0:T(128)S(1)} %copy-done, f32[48,64,2048]{2,1,0:T(8,128)} %volume.13, f32[48,1,2048]{2,1,0:T(1,128)S(1)} %collective-permute-done.2.refs_0_.refs_2_, f32[48,1,2048]{2,1,0:T(1,128)S(1)} %collective-permute-done.3.refs_1_.refs_3_), custom_call_target="tpu_custom_call" | custom-call | tf_op jit(solution)/shard_map/pallas_call | solution.py:365
  26.3 0.0 collective-permute-done.refs_0_
  26.3 0.0 collective-permute-done.1.refs_1_
  26.4 9.6 %shard_map.31 = f32[3,64,512]{2,1,0:T(8,128)S(1)} custom-call(f32[8]{0:T(128)S(1)} %copy-done, f32[48,64,2048]{2,1,0:T(8,128)} %volume.13, f32[1,64,2048]{2,1,0:T(8,128)S(1)} %collective-permute-done.refs_0_, f32[1,64,2048]{2,1,0:T(8,128)S(1)} %collective-permute-done.1.refs_1_, f32[48,1,2048]{2,1,0:T(1,128)S(1)} %collective-permute-done.2.refs_0_.refs_2_, ...), custom_call_target="tpu_custom_call" | custom-call | tf_op jit(solution)/shard_map/pallas_call | solution.py:365
  36.0 2.4 %collective-permute-start.5 = (f32[3,64,512]{2,1,0:T(8,128)S(1)}, f32[3,64,512]{2,1,0:T(8,128)S(1)}, u32[]{:S(2)}, u32[]{:S(2)}) collective-permute-start(f32[3,64,512]{2,1,0:T(8,128)S(1)} %shard_map.31), channel_id=1, source_target_pairs={{0,8},{8,16},{16,24},{24,0},{1,9},{9,17},{17,25},{25,1},{2,10},{10... | collective-permute-start | bytes 1179656 | tf_op jit(solution)/shard_map/ppermute | solution.py:461
  38.4 9.6 %shard_map.32 = f32[3,64,512]{2,1,0:T(8,128)S(1)} custom-call(f32[8]{0:T(128)S(1)} %copy-done, f32[48,64,2048]{2,1,0:T(8,128)} %volume.13, f32[1,64,2048]{2,1,0:T(8,128)S(1)} %collective-permute-done.refs_0_, f32[1,64,2048]{2,1,0:T(8,128)S(1)} %collective-permute-done.1.refs_1_, f32[48,1,2048]{2,1,0:T(1,128)S(1)} %collective-permute-done.2.refs_0_.refs_2_, ...), custom_call_target="tpu_custom_call" | custom-call | tf_op jit(solution)/shard_map/pallas_call | solution.py:365
  48.0 1.8 %collective-permute-start.6 = (f32[3,64,512]{2,1,0:T(8,128)S(1)}, f32[3,64,512]{2,1,0:T(8,128)S(1)}, u32[]{:S(2)}, u32[]{:S(2)}) collective-permute-start(f32[3,64,512]{2,1,0:T(8,128)S(1)} %shard_map.32), channel_id=1, source_target_pairs={{0,24},{8,0},{16,8},{24,16},{1,25},{9,1},{17,9},{25,17},{2,26},{10... | collective-permute-start | bytes 1179656 | tf_op jit(solution)/shard_map/ppermute | solution.py:461
  49.9 2.5 %shard_map.30 = f32[3,64,512]{2,1,0:T(8,128)S(1)} custom-call(f32[8]{0:T(128)S(1)} %copy-done, f32[48,64,2048]{2,1,0:T(8,128)} %volume.13, f32[1,64,2048]{2,1,0:T(8,128)S(1)} %collective-permute-done.refs_0_, f32[1,64,2048]{2,1,0:T(8,128)S(1)} %collective-permute-done.1.refs_1_, f32[48,1,2048]{2,1,0:T(1,128)S(1)} %collective-permute-done.2.refs_0_.refs_2_, ...), custom_call_target="tpu_custom_call" | custom-call | tf_op jit(solution)/shard_map/pallas_call | solution.py:365
  52.4 0.3 collective-permute-start.4
  52.7 9.4 %shard_map.33.refs_3_ = f32[3,64,512]{2,1,0:T(8,128)S(1)} custom-call(f32[8]{0:T(128)S(1)} %copy-done, f32[48,64,2048]{2,1,0:T(8,128)} %volume.13, f32[1,64,2048]{2,1,0:T(8,128)S(1)} %collective-permute-done.refs_0_, f32[1,64,2048]{2,1,0:T(8,128)S(1)} %collective-permute-done.1.refs_1_, f32[48,1,2048]{2,1,0:T(1,128)S(1)} %collective-permute-done.2.refs_0_.refs_2_, ...), custom_call_target="tpu_custom_call" | custom-call | tf_op jit(solution)/shard_map/pallas_call | solution.py:365
  62.0 0.0 collective-permute-done.5.refs_1_
  62.1 0.0 collective-permute-done.6.refs_2_
  62.1 14.5 %collective-permute-done.4.refs_0_ = f32[3,64,512]{2,1,0:T(8,128)S(1)} collective-permute-done((f32[3,64,512]{2,1,0:T(8,128)S(1)}, f32[3,64,512]{2,1,0:T(8,128)S(1)}, u32[]{:S(2)}, u32[]{:S(2)}) %collective-permute-start.4) | collective-permute-done | bytes 393248 | tf_op jit(solution)/shard_map/ppermute | solution.py:461
  76.5 1.7 %merge.1 = f32[4,64,512]{2,1,0:T(8,128)} custom-call(f32[8]{0:T(128)S(1)} %copy-done, f32[3,64,512]{2,1,0:T(8,128)S(1)} %collective-permute-done.4.refs_0_, f32[3,64,512]{2,1,0:T(8,128)S(1)} %collective-permute-done.5.refs_1_, f32[3,64,512]{2,1,0:T(8,128)S(1)} %collective-permute-done.6.refs_2_, f32[3,64,512]{2,1,0:T(8,128)S(1)} %shard_map.33.refs_3_), custom_call_target="tpu_custom_call" | custom-call | tf_op jit(solution)/shard_map/merge/pallas_call | solution.py:420
Async XLA Ops:
  0.0 13.2 %copy-start = (f32[8]{0:T(128)S(1)}, f32[8]{0:T(128)}, u32[]{:S(2)}) copy-start(f32[8]{0:T(128)} %transfer.13) | copy-start | bytes 100
  2.7 23.6 %collective-permute-start = (f32[1,64,2048]{2,1,0:T(8,128)}, f32[1,64,2048]{2,1,0:T(8,128)S(1)}, u32[]{:S(2)}, u32[]{:S(2)}) collective-permute-start(f32[1,64,2048]{2,1,0:T(8,128)} %get-tuple-element.9), channel_id=1, source_target_pairs={{0,8},{8,16},{16,24},{1,9},{9,17},{17,25},{2,10},{10,18},{18,26},{... | collective-permute-start | bytes 1572872 | tf_op jit(solution)/shard_map/ppermute | solution.py:56
  6.0 20.4 %collective-permute-start.1 = (f32[1,64,2048]{2,1,0:T(8,128)}, f32[1,64,2048]{2,1,0:T(8,128)S(1)}, u32[]{:S(2)}, u32[]{:S(2)}) collective-permute-start(f32[1,64,2048]{2,1,0:T(8,128)} %get-tuple-element.10), channel_id=1, source_target_pairs={{8,0},{16,8},{24,16},{9,1},{17,9},{25,17},{10,2},{18,10},{26,18},{... | collective-permute-start | bytes 1572872 | tf_op jit(solution)/shard_map/ppermute | solution.py:56
  7.3 13.6 %collective-permute-start.2 = (f32[48,1,2048]{2,1,0:T(1,128)}, f32[48,1,2048]{2,1,0:T(1,128)S(1)}, u32[]{:S(2)}, u32[]{:S(2)}) collective-permute-start(f32[48,1,2048]{2,1,0:T(1,128)} %get-tuple-element.11), channel_id=1, source_target_pairs={{0,1},{1,2},{2,3},{3,4},{4,5},{5,6},{6,7},{8,9},{9,10},{10,11},{11... | collective-permute-start | bytes 1179656 | tf_op jit(solution)/shard_map/ppermute | solution.py:56
  11.2 10.8 %collective-permute-start.3 = (f32[48,1,2048]{2,1,0:T(1,128)}, f32[48,1,2048]{2,1,0:T(1,128)S(1)}, u32[]{:S(2)}, u32[]{:S(2)}) collective-permute-start(f32[48,1,2048]{2,1,0:T(1,128)} %get-tuple-element.12), channel_id=1, source_target_pairs={{1,0},{2,1},{3,2},{4,3},{5,4},{6,5},{7,6},{9,8},{10,9},{11,10},{12... | collective-permute-start | bytes 1179656 | tf_op jit(solution)/shard_map/ppermute | solution.py:56
  36.0 26.1 %collective-permute-start.5 = (f32[3,64,512]{2,1,0:T(8,128)S(1)}, f32[3,64,512]{2,1,0:T(8,128)S(1)}, u32[]{:S(2)}, u32[]{:S(2)}) collective-permute-start(f32[3,64,512]{2,1,0:T(8,128)S(1)} %shard_map.31), channel_id=1, source_target_pairs={{0,8},{8,16},{16,24},{24,0},{1,9},{9,17},{17,25},{25,1},{2,10},{10... | collective-permute-start | bytes 1179656 | tf_op jit(solution)/shard_map/ppermute | solution.py:461
  48.0 14.0 %collective-permute-start.6 = (f32[3,64,512]{2,1,0:T(8,128)S(1)}, f32[3,64,512]{2,1,0:T(8,128)S(1)}, u32[]{:S(2)}, u32[]{:S(2)}) collective-permute-start(f32[3,64,512]{2,1,0:T(8,128)S(1)} %shard_map.32), channel_id=1, source_target_pairs={{0,24},{8,0},{16,8},{24,16},{1,25},{9,1},{17,9},{25,17},{2,26},{10... | collective-permute-start | bytes 1179656 | tf_op jit(solution)/shard_map/ppermute | solution.py:461
  52.4 24.2 %collective-permute-start.4 = (f32[3,64,512]{2,1,0:T(8,128)S(1)}, f32[3,64,512]{2,1,0:T(8,128)S(1)}, u32[]{:S(2)}, u32[]{:S(2)}) collective-permute-start(f32[3,64,512]{2,1,0:T(8,128)S(1)} %shard_map.30), channel_id=1, source_target_pairs={{0,16},{8,24},{16,0},{24,8},{1,17},{9,25},{17,1},{25,9},{2,18},{10... | collective-permute-start | bytes 1179656 | tf_op jit(solution)/shard_map/ppermute | solution.py:461

commit v6 on v4

--- a/solution.py
+++ b/solution.py
@@ -388,9 +388,9 @@
     )(transfer, *parts)
 
 
-def fold_kernel(own, passed, out):
+def fold_kernel(lower_half, own, passed, out):
     rows, width = out.shape[1:]
-    from_front = lax.axis_index("depth") < lax.axis_size("depth") // 2
+    from_front = (lax.axis_index("depth") < lax.axis_size("depth") // 2) == lower_half
 
     def band(r, carry):
         here = pl.ds(pl.multiple_of(r * SUBLANES, SUBLANES), SUBLANES)
@@ -408,9 +408,9 @@
     lax.fori_loop(0, rows // SUBLANES, band, 0)
 
 
-def fold(own, passed):
+def fold(own, passed, lower_half=True):
     return pl.pallas_call(
-        fold_kernel,
+        functools.partial(fold_kernel, lower_half),
         in_specs=[VMEM, VMEM],
         out_specs=VMEM,
         out_shape=jax.ShapeDtypeStruct(own.shape, jnp.float32),
@@ -419,8 +419,7 @@
     )(own, passed)
 
 
-def exchange(part, groups, flip, members=None):
-    pairs = [(i, i ^ flip) for i in range(groups) if members is None or i in members]
+def send(part, pairs):
     return lax.ppermute(part, "depth", pairs)
 
 
@@ -446,25 +445,33 @@
         (0, 2, SUBLANES, rows - 2 * SUBLANES),
         (slices - 2, 2, SUBLANES, rows - 2 * SUBLANES),
     ]
+
+    def stage(index, flip):
+        if index:
+            kernel = functools.partial(full_kernel, flip, 8, halves, total_slices)
+            return render(kernel, halves, transfer, volume, edges, width, True)
+        kernel = functools.partial(inner_kernel, flip, halves, total_slices)
+        inner = render(kernel, halves, transfer, volume, (), width, False)
+        kernel = functools.partial(rest_kernel, flip, ring, total_slices)
+        return render(kernel, ring, transfer, volume, edges + (inner,), width, True)
+
+    if groups == 4:
+        inward, middle = [(0, 1), (3, 2)], [(1, 2), (2, 1)]
+        far = stage(0, 3)
+        passed = send(far, inward)
+        second = fold(stage(1, 2), passed)
+        from_outer = send(second, inward)
+        from_inner = send(second, middle)
+        third = fold(stage(2, 1), from_inner, False)
+        beside = send(third, [(i, i ^ 1) for i in range(groups)])
+        across = send(fold(far, from_outer), middle)
+        return merge([across, beside, stage(3, 0)], [3, 1, 0], transfer)
+    parts = []
     flips = list(range(groups - 1, -1, -1))
-    hop = groups == 4
-    parts = []
-    for stage, flip in enumerate(flips):
-        if stage == 0:
-            kernel = functools.partial(inner_kernel, flip, halves, total_slices)
-            inner = render(kernel, halves, transfer, volume, (), width, False)
-            kernel = functools.partial(rest_kernel, flip, ring, total_slices)
-            part = render(kernel, ring, transfer, volume, edges + (inner,), width, True)
-        else:
-            kernel = functools.partial(full_kernel, flip, 8, halves, total_slices)
-            part = render(kernel, halves, transfer, volume, edges, width, True)
-        if hop and stage == 0:
-            passed = lax.ppermute(part, "depth", [(0, 1), (3, 2)])
-            part = exchange(part, groups, flip, (1, 2))
-        elif flip:
-            if hop and stage == 1:
-                part = fold(part, passed)
-            part = exchange(part, groups, flip)
+    for index, flip in enumerate(flips):
+        part = stage(index, flip)
+        if flip:
+            part = send(part, [(i, i ^ flip) for i in range(groups)])
         parts.append(part)
     return merge(parts, flips, transfer)
 

time: 75.9 us -> 71.9 us (0.947)
  the two profiles are of different devices: /device:TPU:0 before, /device:TPU:10 now
where the time goes in v6:
time: 71.9 us; the launch traced here: 71.6 us
  Pallas kernels  45.3 us (63%)
  starting transfers between devices  22.8 us (32%)
  waiting for transfers between devices  3.27 us (5%)
    pallas_call x5, Pallas kernels, render(): pl.pallas_call(kernel, in_specs=[SMEM, ANY] + [ANY] * min(4, len(extra))...  40.6 us
    ppermute x4, starting transfers between devices, pass_on(): return lax.ppermute(value, axis, pairs)  11.4 us
    ppermute x5, starting transfers between devices, send(): return lax.ppermute(part, 'depth', pairs)  11.4 us
    ppermute x5, waiting for transfers between devices, send(): return lax.ppermute(part, 'depth', pairs)  3.26 us
    pallas_call x1, Pallas kernels, cut(): pl.pallas_call(cut_kernel, in_specs=[ANY], out_specs=[VMEM] * 4, out_shap...  2.72 us
    pallas_call x1, Pallas kernels, merge(): pl.pallas_call(functools.partial(merge_kernel, flips), in_specs=[SMEM] +...  1.64 us
  transfers between devices with their start and end apart: 9, of which 2 were waited for; matrix products, arithmetic and copies ran while one was open for 0% of the time, Pallas kernels for 51%

profile of v6, /device:TPU:10, one launch (start us, length us, event | category | flops | bytes accessed | tf_op | source)
XLA Modules:
  0.0 71.6 jit_solution(5015351362841513028)
XLA Ops:
  0.0 0.0 copy-start
  0.0 2.7 %cut.1 = (f32[1,64,2048]{2,1,0:T(8,128)}, f32[1,64,2048]{2,1,0:T(8,128)}, f32[48,1,2048]{2,1,0:T(1,128)}, f32[48,1,2048]{2,1,0:T(1,128)}) custom-call(f32[48,64,2048]{2,1,0:T(8,128)} %volume.11), custom_call_target="tpu_custom_call" | custom-call | tf_op jit(solution)/shard_map/cut/pallas_call | solution.py:43
  2.7 3.5 %collective-permute-start = (f32[1,64,2048]{2,1,0:T(8,128)}, f32[1,64,2048]{2,1,0:T(8,128)S(1)}, u32[]{:S(2)}, u32[]{:S(2)}) collective-permute-start(f32[1,64,2048]{2,1,0:T(8,128)} %get-tuple-element.9), channel_id=1, source_target_pairs={{0,8},{8,16},{16,24},{1,9},{9,17},{17,25},{2,10},{10,18},{18,26},{... | collective-permute-start | bytes 1572872 | tf_op jit(solution)/shard_map/ppermute | solution.py:56
  6.2 2.4 %collective-permute-start.1 = (f32[1,64,2048]{2,1,0:T(8,128)}, f32[1,64,2048]{2,1,0:T(8,128)S(1)}, u32[]{:S(2)}, u32[]{:S(2)}) collective-permute-start(f32[1,64,2048]{2,1,0:T(8,128)} %get-tuple-element.10), channel_id=1, source_target_pairs={{8,0},{16,8},{24,16},{9,1},{17,9},{25,17},{10,2},{18,10},{26,18},{... | collective-permute-start | bytes 1572872 | tf_op jit(solution)/shard_map/ppermute | solution.py:56
  8.6 1.9 %collective-permute-start.2 = (f32[48,1,2048]{2,1,0:T(1,128)}, f32[48,1,2048]{2,1,0:T(1,128)S(1)}, u32[]{:S(2)}, u32[]{:S(2)}) collective-permute-start(f32[48,1,2048]{2,1,0:T(1,128)} %get-tuple-element.11), channel_id=1, source_target_pairs={{0,1},{1,2},{2,3},{3,4},{4,5},{5,6},{6,7},{8,9},{9,10},{10,11},{11... | collective-permute-start | bytes 1179656 | tf_op jit(solution)/shard_map/ppermute | solution.py:56
  10.5 3.6 %collective-permute-start.3 = (f32[48,1,2048]{2,1,0:T(1,128)}, f32[48,1,2048]{2,1,0:T(1,128)S(1)}, u32[]{:S(2)}, u32[]{:S(2)}) collective-permute-start(f32[48,1,2048]{2,1,0:T(1,128)} %get-tuple-element.12), channel_id=1, source_target_pairs={{1,0},{2,1},{3,2},{4,3},{5,4},{6,5},{7,6},{9,8},{10,9},{11,10},{12... | collective-permute-start | bytes 1179656 | tf_op jit(solution)/shard_map/ppermute | solution.py:56
  14.2 0.0 copy-done
  14.2 7.7 %shard_map.28.refs_4_ = f32[3,64,512]{2,1,0:T(8,128)S(1)} custom-call(f32[8]{0:T(128)S(1)} %copy-done, f32[48,64,2048]{2,1,0:T(8,128)} %volume.11), custom_call_target="tpu_custom_call" | custom-call | tf_op jit(solution)/shard_map/pallas_call | solution.py:333
  21.9 0.0 collective-permute-done.2.refs_2_
  21.9 0.0 collective-permute-done.3.refs_3_
  21.9 0.0 collective-permute-done.refs_0_
  21.9 0.0 collective-permute-done.1.refs_1_
  21.9 4.6 %shard_map.29.own = f32[3,64,512]{2,1,0:T(8,128)S(1)} custom-call(f32[8]{0:T(128)S(1)} %copy-done, f32[48,64,2048]{2,1,0:T(8,128)} %volume.11, f32[1,64,2048]{2,1,0:T(8,128)S(1)} %collective-permute-done.refs_0_, f32[1,64,2048]{2,1,0:T(8,128)S(1)} %collective-permute-done.1.refs_1_, f32[48,1,2048]{2,1,0:T(1,128)S(1)} %collective-permute-done.2.refs_2_, ...), custom_call_target="tpu_custom_call" | custom-call | tf_op jit(solution)/shard_map/pallas_call | solution.py:333
  26.5 1.3 %collective-permute-start.4 = (f32[3,64,512]{2,1,0:T(8,128)S(1)}, f32[3,64,512]{2,1,0:T(8,128)S(1)}, u32[]{:S(2)}, u32[]{:S(2)}) collective-permute-start(f32[3,64,512]{2,1,0:T(8,128)S(1)} %shard_map.29.own), channel_id=1, source_target_pairs={{0,8},{24,16},{1,9},{25,17},{2,10},{26,18},{3,11},{27,19},{4,12},{... | collective-permute-start | bytes 1179656 | tf_op jit(solution)/shard_map/ppermute | solution.py:423
  27.8 9.5 %shard_map.30.own = f32[3,64,512]{2,1,0:T(8,128)S(1)} custom-call(f32[8]{0:T(128)S(1)} %copy-done, f32[48,64,2048]{2,1,0:T(8,128)} %volume.11, f32[1,64,2048]{2,1,0:T(8,128)S(1)} %collective-permute-done.refs_0_, f32[1,64,2048]{2,1,0:T(8,128)S(1)} %collective-permute-done.1.refs_1_, f32[48,1,2048]{2,1,0:T(1,128)S(1)} %collective-permute-done.2.refs_2_, ...), custom_call_target="tpu_custom_call" | custom-call | tf_op jit(solution)/shard_map/pallas_call | solution.py:333
  37.4 3.0 %collective-permute-done.4.passed = f32[3,64,512]{2,1,0:T(8,128)S(1)} collective-permute-done((f32[3,64,512]{2,1,0:T(8,128)S(1)}, f32[3,64,512]{2,1,0:T(8,128)S(1)}, u32[]{:S(2)}, u32[]{:S(2)}) %collective-permute-start.4) | collective-permute-done | bytes 393248 | tf_op jit(solution)/shard_map/ppermute | solution.py:423
  40.4 0.1 fold.3
  40.5 3.5 %collective-permute-start.7 = (f32[3,64,512]{2,1,0:T(8,128)S(1)}, f32[3,64,512]{2,1,0:T(8,128)S(1)}, u32[]{:S(2)}, u32[]{:S(2)}) collective-permute-start(f32[3,64,512]{2,1,0:T(8,128)S(1)} %fold.3), channel_id=1, source_target_pairs={{8,16},{16,8},{9,17},{17,9},{10,18},{18,10},{11,19},{19,11},{12,20... | collective-permute-start | bytes 1179656 | tf_op jit(solution)/shard_map/ppermute | solution.py:423
  43.9 1.3 %collective-permute-start.5 = (f32[3,64,512]{2,1,0:T(8,128)S(1)}, f32[3,64,512]{2,1,0:T(8,128)S(1)}, u32[]{:S(2)}, u32[]{:S(2)}) collective-permute-start(f32[3,64,512]{2,1,0:T(8,128)S(1)} %fold.3), channel_id=1, source_target_pairs={{0,8},{24,16},{1,9},{25,17},{2,10},{26,18},{3,11},{27,19},{4,12},{... | collective-permute-start | bytes 1179656 | tf_op jit(solution)/shard_map/ppermute | solution.py:423
  45.2 9.3 %shard_map.31.own = f32[3,64,512]{2,1,0:T(8,128)S(1)} custom-call(f32[8]{0:T(128)S(1)} %copy-done, f32[48,64,2048]{2,1,0:T(8,128)} %volume.11, f32[1,64,2048]{2,1,0:T(8,128)S(1)} %collective-permute-done.refs_0_, f32[1,64,2048]{2,1,0:T(8,128)S(1)} %collective-permute-done.1.refs_1_, f32[48,1,2048]{2,1,0:T(1,128)S(1)} %collective-permute-done.2.refs_2_, ...), custom_call_target="tpu_custom_call" | custom-call | tf_op jit(solution)/shard_map/pallas_call | solution.py:333
  54.5 0.0 collective-permute-done.7.passed
  54.5 0.1 fold.5
  54.6 3.0 %collective-permute-start.8 = (f32[3,64,512]{2,1,0:T(8,128)S(1)}, f32[3,64,512]{2,1,0:T(8,128)S(1)}, u32[]{:S(2)}, u32[]{:S(2)}) collective-permute-start(f32[3,64,512]{2,1,0:T(8,128)S(1)} %fold.5), channel_id=1, source_target_pairs={{0,8},{8,0},{16,24},{24,16},{1,9},{9,1},{17,25},{25,17},{2,10},{10... | collective-permute-start | bytes 1179656 | tf_op jit(solution)/shard_map/ppermute | solution.py:423
  57.6 0.0 collective-permute-done.5.passed
  57.6 0.1 fold.4
  57.7 2.4 %collective-permute-start.6 = (f32[3,64,512]{2,1,0:T(8,128)S(1)}, f32[3,64,512]{2,1,0:T(8,128)S(1)}, u32[]{:S(2)}, u32[]{:S(2)}) collective-permute-start(f32[3,64,512]{2,1,0:T(8,128)S(1)} %fold.4), channel_id=1, source_target_pairs={{8,16},{16,8},{9,17},{17,9},{10,18},{18,10},{11,19},{19,11},{12,20... | collective-permute-start | bytes 1179656 | tf_op jit(solution)/shard_map/ppermute | solution.py:423
  60.1 9.5 %shard_map.32.refs_2_ = f32[3,64,512]{2,1,0:T(8,128)S(1)} custom-call(f32[8]{0:T(128)S(1)} %copy-done, f32[48,64,2048]{2,1,0:T(8,128)} %volume.11, f32[1,64,2048]{2,1,0:T(8,128)S(1)} %collective-permute-done.refs_0_, f32[1,64,2048]{2,1,0:T(8,128)S(1)} %collective-permute-done.1.refs_1_, f32[48,1,2048]{2,1,0:T(1,128)S(1)} %collective-permute-done.2.refs_2_, ...), custom_call_target="tpu_custom_call" | custom-call | tf_op jit(solution)/shard_map/pallas_call | solution.py:333
  69.7 0.0 collective-permute-done.8.refs_1_
  69.7 0.2 collective-permute-done.6.refs_0_
  69.9 1.6 %merge.1 = f32[4,64,512]{2,1,0:T(8,128)} custom-call(f32[8]{0:T(128)S(1)} %copy-done, f32[3,64,512]{2,1,0:T(8,128)S(1)} %collective-permute-done.6.refs_0_, f32[3,64,512]{2,1,0:T(8,128)S(1)} %collective-permute-done.8.refs_1_, f32[3,64,512]{2,1,0:T(8,128)S(1)} %shard_map.32.refs_2_), custom_call_target="tpu_custom_call" | custom-call | tf_op jit(solution)/shard_map/merge/pallas_call | solution.py:381
Async XLA Ops:
  0.0 14.2 %copy-start = (f32[8]{0:T(128)S(1)}, f32[8]{0:T(128)}, u32[]{:S(2)}) copy-start(f32[8]{0:T(128)} %transfer.11) | copy-start | bytes 100
  2.7 19.2 %collective-permute-start = (f32[1,64,2048]{2,1,0:T(8,128)}, f32[1,64,2048]{2,1,0:T(8,128)S(1)}, u32[]{:S(2)}, u32[]{:S(2)}) collective-permute-start(f32[1,64,2048]{2,1,0:T(8,128)} %get-tuple-element.9), channel_id=1, source_target_pairs={{0,8},{8,16},{16,24},{1,9},{9,17},{17,25},{2,10},{10,18},{18,26},{... | collective-permute-start | bytes 1572872 | tf_op jit(solution)/shard_map/ppermute | solution.py:56
  6.2 15.7 %collective-permute-start.1 = (f32[1,64,2048]{2,1,0:T(8,128)}, f32[1,64,2048]{2,1,0:T(8,128)S(1)}, u32[]{:S(2)}, u32[]{:S(2)}) collective-permute-start(f32[1,64,2048]{2,1,0:T(8,128)} %get-tuple-element.10), channel_id=1, source_target_pairs={{8,0},{16,8},{24,16},{9,1},{17,9},{25,17},{10,2},{18,10},{26,18},{... | collective-permute-start | bytes 1572872 | tf_op jit(solution)/shard_map/ppermute | solution.py:56
  8.6 13.3 %collective-permute-start.2 = (f32[48,1,2048]{2,1,0:T(1,128)}, f32[48,1,2048]{2,1,0:T(1,128)S(1)}, u32[]{:S(2)}, u32[]{:S(2)}) collective-permute-start(f32[48,1,2048]{2,1,0:T(1,128)} %get-tuple-element.11), channel_id=1, source_target_pairs={{0,1},{1,2},{2,3},{3,4},{4,5},{5,6},{6,7},{8,9},{9,10},{10,11},{11... | collective-permute-start | bytes 1179656 | tf_op jit(solution)/shard_map/ppermute | solution.py:56
  10.5 11.3 %collective-permute-start.3 = (f32[48,1,2048]{2,1,0:T(1,128)}, f32[48,1,2048]{2,1,0:T(1,128)S(1)}, u32[]{:S(2)}, u32[]{:S(2)}) collective-permute-start(f32[48,1,2048]{2,1,0:T(1,128)} %get-tuple-element.12), channel_id=1, source_target_pairs={{1,0},{2,1},{3,2},{4,3},{5,4},{6,5},{7,6},{9,8},{10,9},{11,10},{12... | collective-permute-start | bytes 1179656 | tf_op jit(solution)/shard_map/ppermute | solution.py:56
  26.5 13.8 %collective-permute-start.4 = (f32[3,64,512]{2,1,0:T(8,128)S(1)}, f32[3,64,512]{2,1,0:T(8,128)S(1)}, u32[]{:S(2)}, u32[]{:S(2)}) collective-permute-start(f32[3,64,512]{2,1,0:T(8,128)S(1)} %shard_map.29.own), channel_id=1, source_target_pairs={{0,8},{24,16},{1,9},{25,17},{2,10},{26,18},{3,11},{27,19},{4,12},{... | collective-permute-start | bytes 1179656 | tf_op jit(solution)/shard_map/ppermute | solution.py:423
  40.5 14.0 %collective-permute-start.7 = (f32[3,64,512]{2,1,0:T(8,128)S(1)}, f32[3,64,512]{2,1,0:T(8,128)S(1)}, u32[]{:S(2)}, u32[]{:S(2)}) collective-permute-start(f32[3,64,512]{2,1,0:T(8,128)S(1)} %fold.3), channel_id=1, source_target_pairs={{8,16},{16,8},{9,17},{17,9},{10,18},{18,10},{11,19},{19,11},{12,20... | collective-permute-start | bytes 1179656 | tf_op jit(solution)/shard_map/ppermute | solution.py:423
  43.9 13.7 %collective-permute-start.5 = (f32[3,64,512]{2,1,0:T(8,128)S(1)}, f32[3,64,512]{2,1,0:T(8,128)S(1)}, u32[]{:S(2)}, u32[]{:S(2)}) collective-permute-start(f32[3,64,512]{2,1,0:T(8,128)S(1)} %fold.3), channel_id=1, source_target_pairs={{0,8},{24,16},{1,9},{25,17},{2,10},{26,18},{3,11},{27,19},{4,12},{... | collective-permute-start | bytes 1179656 | tf_op jit(solution)/shard_map/ppermute | solution.py:423
  54.6 15.0 %collective-permute-start.8 = (f32[3,64,512]{2,1,0:T(8,128)S(1)}, f32[3,64,512]{2,1,0:T(8,128)S(1)}, u32[]{:S(2)}, u32[]{:S(2)}) collective-permute-start(f32[3,64,512]{2,1,0:T(8,128)S(1)} %fold.5), channel_id=1, source_target_pairs={{0,8},{8,0},{16,24},{24,16},{1,9},{9,1},{17,25},{25,17},{2,10},{10... | collective-permute-start | bytes 1179656 | tf_op jit(solution)/shard_map/ppermute | solution.py:423
  57.7 12.2 %collective-permute-start.6 = (f32[3,64,512]{2,1,0:T(8,128)S(1)}, f32[3,64,512]{2,1,0:T(8,128)S(1)}, u32[]{:S(2)}, u32[]{:S(2)}) collective-permute-start(f32[3,64,512]{2,1,0:T(8,128)S(1)} %fold.4), channel_id=1, source_target_pairs={{8,16},{16,8},{9,17},{17,9},{10,18},{18,10},{11,19},{19,11},{12,20... | collective-permute-start | bytes 1179656 | tf_op jit(solution)/shard_map/ppermute | solution.py:423
